TPU v7x, 32 devices: a whole 2x2x4 slice. The times are simulated.
32 devices in a mesh: mem: 4 (over y, x), grid: 8 (over z, core).
Axes of the slice: x: 2, y: 2, z: 4, core: 2. Of those that a mesh axis runs over, the one named last changes fastest.
Arguments:
- initial_concentrations: float32 [16, 4, 768, 1536], P('mem', None, 'grid'), may hold values from 0.5 to 2
- rate_field: bfloat16 [12, 768, 1536], P(None, 'grid'), may hold values from 0.019897461 to 0.29882812
- kinetic_scaling_factors: bfloat16 [16, 12, 256, 6], P('mem', None, 'grid'), may hold values from 0.5 to 2
- observed_cell: int32 [256, 6, 128], P('grid'), may hold values from 0 to 3071
- measured_value: float32 [256, 6, 128], P('grid'), may hold values from 0.5 to 2
- error_variance: float32 [256, 6, 128], P('grid'), may hold values from 0.05 to 0.5
Outputs:
- analysis: bfloat16 [16, 4, 768, 1536], P('mem', None, 'grid')
- mult_analysis: bfloat16 [16, 12, 256, 6], P('mem', None, 'grid')
Inputs may be any that keep to these rules, and one draw needn't show every extreme that they name: `observed_cell`: an observation's entry is tracer * 3 * 256 + row * 256 + column within its patch.
All inputs are finite; a program needn't handle non-finite values.
Results may differ from a plain program's by a relative error of at most 0.011.
The roundings to bfloat16 on the way count: a program that leaves them out, or rounds other values in their place, can miss the bound.
Values may be sent and summed in bfloat16 or wider, within the bound.
No kernel may reach another device: no remote copies, remote signals or barrier semaphores. Data moves between devices by JAX's collectives and lax.ppermute only.
A program may use at most 192 MiB of HBM per device.

v0:
```python
import functools
import math

import jax
import jax.numpy as jnp
from jax import lax
from jax.experimental import pallas as pl
from jax.experimental.pallas import tpu as pltpu
from jax.sharding import PartitionSpec as P

NW = 512
PLAT = 3
PLON = 256
SWEEPS = 5
LANES = 128
SUBLANES = 8

damping = 2.0
f32 = jnp.float32
bf16 = jnp.bfloat16


def rounded_angle(product, period):
    turns = jnp.floor(product * (1.0 / period))
    return (product - turns * period) * (2.0 * math.pi / period)


def forward_kernel(bands, waves, x_ref, o_ref, table, coarse, fine):
    tracers, band, longitudes = x_ref.shape[1:]
    columns = table.shape[1]
    local = 2 * waves
    step = fine.shape[1]

    @pl.when(pl.program_id(0) == 0)
    def _():
        def waves_of(rows):
            q = lax.broadcasted_iota(jnp.int32, (rows, columns), 1)
            p = q // local
            part = (q % local) // waves
            wave = bands * (q % waves) + p
            return wave.astype(f32), part

        rows = coarse.shape[1]
        wave, part = waves_of(rows)
        row = lax.broadcasted_iota(jnp.int32, (rows, columns), 0) * step
        angle = rounded_angle(wave * row.astype(f32), longitudes)
        cosine, sine = jnp.cos(angle), jnp.sin(angle)
        coarse[0] = jnp.where(part == 0, cosine, -sine)
        coarse[1] = jnp.where(part == 0, sine, cosine)
        wave, part = waves_of(step)
        row = lax.broadcasted_iota(jnp.int32, (step, columns), 0)
        angle = rounded_angle(wave * row.astype(f32), longitudes)
        fine[0] = jnp.cos(angle)
        fine[1] = jnp.sin(angle)

        def build(at, carry):
            block = coarse[0, pl.ds(at, 1), :] * fine[0] - coarse[1, pl.ds(at, 1), :] * fine[1]
            start = pl.multiple_of(at * step, step)
            table[pl.ds(start, step), :] = block.astype(bf16)
            return carry

        lax.fori_loop(0, rows, build, 0)

    x = x_ref[0].astype(bf16).reshape(tracers * band, longitudes)
    y = jnp.dot(x, table[...], preferred_element_type=f32) * (1.0 / longitudes)
    y = y.astype(bf16).reshape(tracers, band, columns)
    for t in range(tracers):
        for p in range(bands):
            o_ref[p, :, t * local : (t + 1) * local] = y[t, :, p * local : (p + 1) * local]


def forward_transform(x, bands, waves):
    group, tracers, band, longitudes = x.shape
    local = 2 * waves
    step = 32 if longitudes % 32 == 0 else 8
    return pl.pallas_call(
        functools.partial(forward_kernel, bands, waves),
        grid=(group,),
        in_specs=[pl.BlockSpec((1, tracers, band, longitudes), lambda g: (g, 0, 0, 0))],
        out_specs=pl.BlockSpec((bands, band, tracers * local), lambda g: (0, 0, g)),
        out_shape=jax.ShapeDtypeStruct((bands, band, group * tracers * local), bf16),
        scratch_shapes=[
            pltpu.VMEM((longitudes, bands * local), bf16),
            pltpu.VMEM((2, longitudes // step, bands * local), f32),
            pltpu.VMEM((2, step, bands * local), f32),
        ],
        compiler_params=pltpu.CompilerParams(vmem_limit_bytes=60 * 2**20),
        name="forward_dft",
    )(x)


def meridional_kernel(waves, a_ref, ahead_ref, back_ref, gain_ref, o_ref):
    local = 2 * waves
    tracers = a_ref.shape[1] // local
    spectrum = jnp.dot(ahead_ref[...], a_ref[...], preferred_element_type=f32)
    gain = jnp.concatenate([gain_ref[...]] * tracers, axis=1)
    damped = (spectrum * gain).astype(bf16)
    back = jnp.dot(back_ref[...], damped, preferred_element_type=f32).astype(bf16)
    owners, _, rows, _ = o_ref.shape
    own = rows // tracers
    for t in range(tracers):
        part = back[:, t * local : (t + 1) * local].reshape(owners, own, local)
        o_ref[:, 0, t * own : (t + 1) * own, :] = part


def meridional_transform(arrived, ahead, back, gain, waves, tracers, owners):
    latitudes, columns = arrived.shape
    local = 2 * waves
    group = columns // (tracers * local)
    own = latitudes // owners
    whole = lambda g: (0, 0)
    return pl.pallas_call(
        functools.partial(meridional_kernel, waves),
        grid=(group,),
        in_specs=[
            pl.BlockSpec((latitudes, tracers * local), lambda g: (0, g)),
            pl.BlockSpec(ahead.shape, whole),
            pl.BlockSpec(back.shape, whole),
            pl.BlockSpec(gain.shape, whole),
        ],
        out_specs=pl.BlockSpec((owners, 1, tracers * own, local), lambda g: (0, g, 0, 0)),
        out_shape=jax.ShapeDtypeStruct((owners, group, tracers * own, local), bf16),
        compiler_params=pltpu.CompilerParams(vmem_limit_bytes=60 * 2**20),
        name="meridional",
    )(arrived, ahead, back, gain)


def meridional_tables(latitudes, own, bands, groups):
    device = lax.axis_index("grid")
    even = device % 2 == 0
    modes = jnp.arange(NW, dtype=jnp.int32)
    order = jnp.where(even, modes, modes + 1).astype(f32)

    def values(theta, order):
        angle = theta * order
        return jnp.where(even, jnp.cos(angle), jnp.sin(angle)).astype(bf16)

    theta = (jnp.arange(latitudes, dtype=f32) + 0.5) * (math.pi / latitudes)
    ahead = values(theta[None, :], order[:, None])
    rows = own // PLAT
    index = (
        lax.broadcasted_iota(jnp.int32, (groups, bands, PLAT, rows), 0) * own
        + lax.broadcasted_iota(jnp.int32, (groups, bands, PLAT, rows), 1) * (own * groups)
        + lax.broadcasted_iota(jnp.int32, (groups, bands, PLAT, rows), 2)
        + lax.broadcasted_iota(jnp.int32, (groups, bands, PLAT, rows), 3) * PLAT
    ).reshape(latitudes)
    theta = (index.astype(f32) + 0.5) * (math.pi / latitudes)
    back = values(theta[:, None], order[None, :])
    return ahead, back


def spectral_gain(latitudes, waves, bands):
    device = lax.axis_index("grid")
    modes = jnp.arange(NW, dtype=jnp.int32)[:, None]
    column = jnp.arange(2 * waves, dtype=jnp.int32)[None, :]
    wave = bands * (column % waves) + device
    total = (wave + modes).astype(f32)
    ratio = total * (total + 1.0) / float(NW * (NW - 1))
    half = jnp.where((wave % 2 == 0) & (modes == 0), 0.5, 1.0)
    gain = half / (1.0 + damping * ratio * ratio)
    return jnp.where(wave + modes <= NW - 1, gain, 0.0) * (2.0 / latitudes)


def inverse_table(longitudes, waves, bands):
    q = jnp.arange(bands * 2 * waves, dtype=jnp.int32)
    device = q // (2 * waves)
    part = (q % (2 * waves)) // waves
    wave = bands * (q % waves) + device
    column = jnp.arange(longitudes, dtype=jnp.int32)
    phase = wave[:, None] * column[None, :] % longitudes
    phase = phase + jnp.where(part == 0, 0, longitudes // 4)[:, None]
    weight = jnp.where(wave == 0, 1.0, 2.0)[:, None]
    angle = phase.astype(f32) * (2.0 * math.pi / longitudes)
    return (weight * jnp.cos(angle)).astype(bf16)


def chemistry_kernel(
    z_ref, table_ref, rate_ref, factor_ref, lane_ref, place_ref, bg_ref, seen_ref, lhs, smooth, fresh
):
    sources, bands, rows, local = z_ref.shape
    reactions, height, patch_rows, _ = rate_ref.shape
    members = factor_ref.shape[1]
    tracers = bg_ref.shape[0]
    others = tracers - 1
    group = members // sources
    own = height * patch_rows

    @pl.when(pl.program_id(0) == 0)
    def _():
        for s in range(sources):
            for p in range(bands):
                lhs[s * rows : (s + 1) * rows, p * local : (p + 1) * local] = z_ref[s, p]

    smooth[...] = jnp.dot(lhs[...], table_ref[...], preferred_element_type=f32).reshape(
        members, tracers, height, patch_rows, PLON
    )

    def one_member(e, carry):
        for i in range(height):
            for at in range(0, PLON, LANES):
                lanes = slice(at, at + LANES)
                rates = [
                    factor_ref[0, e, r] * rate_ref[r, i, :, lanes] for r in range(reactions)
                ]
                moved, kept = [], []
                for a in range(tracers):
                    outflow = rates[others * a]
                    for s in range(1, others):
                        outflow = outflow + rates[others * a + s]
                    kept.append(smooth[e, a, i, :, lanes] * (1.0 / (1.0 + outflow)))
                for b in range(tracers):
                    value = kept[b]
                    for a in range(tracers):
                        if a != b:
                            s = b if b < a else b - 1
                            value = value + rates[others * a + s] * kept[a]
                    fresh[b, i, e, :, lanes] = value
        return carry

    lax.fori_loop(0, members, one_member, 0)
    for t in range(tracers):
        for i in range(height):
            bg_ref[t, i] = fresh[t, i].reshape(members * patch_rows, PLON).astype(bf16)

    copies = max(1, SUBLANES // patch_rows)

    def tiled(array):
        return jnp.concatenate([array] * copies, axis=0) if copies > 1 else array

    lane = tiled(lane_ref[0])
    place = tiled(place_ref[0])
    within = lane % LANES
    piece = lane // LANES

    def observe(e, carry):
        seen = jnp.zeros(lane.shape, f32)
        for t in range(tracers):
            for i in range(height):
                value = tiled(fresh[t, i, e])
                for k in range(PLON // LANES):
                    found = jnp.take_along_axis(
                        value[:, k * LANES : (k + 1) * LANES],
                        within,
                        axis=1,
                        mode="promise_in_bounds",
                    )
                    here = (place == t * height + i) & (piece == k)
                    seen = jnp.where(here, found, seen)
        seen_ref[0, e] = seen[:patch_rows].astype(bf16).astype(f32)
        return carry

    lax.fori_loop(0, members, observe, 0)


def chemistry(z, table, rate, factor, lane, place, tracers):
    sources, bands, rows, local = z.shape
    reactions, height, patch_rows, longitudes = rate.shape
    cols, members = factor.shape[:2]
    observations = lane.shape[-1]
    return pl.pallas_call(
        chemistry_kernel,
        grid=(cols,),
        in_specs=[
            pl.BlockSpec(z.shape, lambda c: (0, 0, 0, 0)),
            pl.BlockSpec((table.shape[0], PLON), lambda c: (0, c)),
            pl.BlockSpec((reactions, height, patch_rows, PLON), lambda c: (0, 0, 0, c)),
            pl.BlockSpec((1, members, reactions, patch_rows, LANES), lambda c: (c, 0, 0, 0, 0)),
            pl.BlockSpec((1, patch_rows, observations), lambda c: (c, 0, 0)),
            pl.BlockSpec((1, patch_rows, observations), lambda c: (c, 0, 0)),
        ],
        out_specs=[
            pl.BlockSpec((tracers, height, members * patch_rows, PLON), lambda c: (0, 0, 0, c)),
            pl.BlockSpec((1, members, patch_rows, observations), lambda c: (c, 0, 0, 0)),
        ],
        out_shape=[
            jax.ShapeDtypeStruct((tracers, height, members * patch_rows, longitudes), bf16),
            jax.ShapeDtypeStruct((cols, members, patch_rows, observations), f32),
        ],
        scratch_shapes=[
            pltpu.VMEM((sources * rows, bands * local), bf16),
            pltpu.VMEM((members, tracers, height, patch_rows, PLON), f32),
            pltpu.VMEM((tracers, height, members, patch_rows, PLON), f32),
        ],
        compiler_params=pltpu.CompilerParams(vmem_limit_bytes=60 * 2**20),
        name="chemistry",
    )(z, table, rate, factor, lane, place)


def apply_kernel(high_ref, low_ref, bg_ref, o_ref, rows):
    members, tracers, own, _ = o_ref.shape
    height = bg_ref.shape[1]
    patch_rows = own // height
    for t in range(tracers):
        for i in range(height):
            value = bg_ref[t, i]
            new = jnp.dot(high_ref[0], value, preferred_element_type=f32)
            new = new + jnp.dot(low_ref[0], value, preferred_element_type=f32)
            for j in range(members):
                part = new[j * patch_rows : (j + 1) * patch_rows]
                for k in range(PLON // LANES):
                    rows[k, j, pl.ds(i, patch_rows, stride=height), :] = part[
                        :, k * LANES : (k + 1) * LANES
                    ]
        for k in range(PLON // LANES):
            o_ref[:, t, :, k * LANES : (k + 1) * LANES] = rows[k].astype(bf16)


def apply_weights(high, low, bg, members, own):
    tracers, height, wide, longitudes = bg.shape
    cols = high.shape[0]
    return pl.pallas_call(
        apply_kernel,
        grid=(cols,),
        in_specs=[
            pl.BlockSpec((1, wide, wide), lambda c: (c, 0, 0)),
            pl.BlockSpec((1, wide, wide), lambda c: (c, 0, 0)),
            pl.BlockSpec((tracers, height, wide, PLON), lambda c: (0, 0, 0, c)),
        ],
        out_specs=pl.BlockSpec((members, tracers, own, PLON), lambda c: (0, 0, 0, c)),
        out_shape=jax.ShapeDtypeStruct((members, tracers, own, longitudes), bf16),
        scratch_shapes=[pltpu.VMEM((PLON // LANES, members, own, LANES), f32)],
        compiler_params=pltpu.CompilerParams(vmem_limit_bytes=60 * 2**20),
        name="apply_weights",
    )(high, low, bg)


def ensemble_transform(predicted, observed, variance):
    highest = lax.Precision.HIGHEST
    members = predicted.shape[1]
    seen_mean = jnp.mean(predicted, axis=1, keepdims=True)
    seen_spread = predicted - seen_mean
    weighted = seen_spread * (1.0 / variance)[:, None, :]
    outer = jnp.einsum("pik,pjk->pij", weighted, seen_spread, precision=highest)
    scale = members - 1.0 + jnp.sqrt(jnp.sum(outer * outer, axis=(1, 2)))
    identity = jnp.eye(members, dtype=f32)
    current = ((members - 1.0) * identity + outer) / scale[:, None, None]
    root = jnp.broadcast_to(identity, current.shape)
    for sweep in range(SWEEPS):
        middle = 1.5 * identity - 0.5 * jnp.einsum("pij,pjk->pik", root, current, precision=highest)
        current = jnp.einsum("pij,pjk->pik", current, middle, precision=highest)
        root = jnp.einsum("pij,pjk->pik", middle, root, precision=highest)
    covariance = jnp.einsum("pij,pjk->pik", root, root, precision=highest) / scale[:, None, None]
    innovation = observed - seen_mean[:, 0, :]
    projected = jnp.einsum("pjk,pk->pj", weighted, innovation, precision=highest)
    coefficient = jnp.einsum("pij,pj->pi", covariance, projected, precision=highest)
    return jnp.sqrt((members - 1.0) / scale)[:, None, None] * root + coefficient[:, :, None]


def on_device(
    initial_concentrations,
    rate_field,
    kinetic_scaling_factors,
    observed_cell,
    measured_value,
    error_variance,
):
    group, tracers, band, longitudes = initial_concentrations.shape
    bands = lax.axis_size("grid")
    groups = lax.axis_size("mem")
    members = group * groups
    reactions = rate_field.shape[0]
    waves = NW // bands
    latitudes = band * bands
    own = band // groups
    patch_rows = own // PLAT
    cols = longitudes // PLON
    mem = lax.axis_index("mem")

    fourier = forward_transform(initial_concentrations, bands, waves)
    arrived = lax.all_to_all(fourier, "grid", split_axis=0, concat_axis=0, tiled=True)

    factors = lax.all_to_all(
        kinetic_scaling_factors.reshape(group, reactions, groups, patch_rows, cols).transpose(
            2, 0, 1, 3, 4
        ),
        "mem",
        split_axis=0,
        concat_axis=0,
        tiled=True,
    ).reshape(members, reactions, patch_rows, cols)
    ahead, back = meridional_tables(latitudes, own, bands, groups)
    gain = spectral_gain(latitudes, waves, bands)
    inverse = inverse_table(longitudes, waves, bands)
    rate = (
        lax.dynamic_slice_in_dim(rate_field, mem * own, own, 1)
        .astype(f32)
        .reshape(reactions, patch_rows, PLAT, longitudes)
        .transpose(0, 2, 1, 3)
    )
    factor = jnp.broadcast_to(
        factors.astype(f32).transpose(3, 0, 1, 2)[..., None],
        (cols, members, reactions, patch_rows, LANES),
    )

    def own_patches(array):
        mine = lax.dynamic_slice_in_dim(array, mem * patch_rows, patch_rows, 0)
        return mine.transpose(1, 0, 2)

    cell = own_patches(observed_cell)
    lane = cell % PLON
    place = cell // PLON
    observed = own_patches(measured_value)
    variance = own_patches(error_variance)

    last = meridional_transform(
        arrived.reshape(latitudes, group * tracers * 2 * waves),
        ahead,
        back,
        gain,
        waves,
        tracers,
        groups * bands,
    )
    returned = lax.all_to_all(last, ("mem", "grid"), split_axis=0, concat_axis=0, tiled=True)
    z = returned.reshape(groups, bands, group * tracers * own, 2 * waves)
    bg, seen = chemistry(z, inverse, rate, factor, lane, place, tracers)

    patches = cols * patch_rows
    predicted = seen.transpose(0, 2, 1, 3).reshape(patches, members, -1)
    transform = ensemble_transform(
        predicted, observed.reshape(patches, -1), variance.reshape(patches, -1)
    )
    weights = transform + (1.0 - jnp.sum(transform, axis=1, keepdims=True)) / members
    weights = weights.reshape(cols, patch_rows, members, members)
    same = jnp.eye(patch_rows, dtype=f32)
    spread = weights.transpose(0, 3, 1, 2)[..., None] * same[None, None, :, None, :]
    spread = spread.reshape(cols, members * patch_rows, members * patch_rows)
    high = spread.astype(bf16)
    low = (spread - high.astype(f32)).astype(bf16)
    analysed = apply_weights(high, low, bg, members, own)
    landed = lax.all_to_all(
        analysed.reshape(groups, group, tracers, own, longitudes),
        "mem",
        split_axis=0,
        concat_axis=0,
        tiled=True,
    )
    analysis = landed.transpose(1, 2, 0, 3, 4).reshape(group, tracers, band, longitudes)

    theta = jnp.log(factors.astype(f32)).transpose(3, 2, 0, 1).reshape(patches, members, reactions)
    theta_mean = jnp.mean(theta, axis=1, keepdims=True)
    theta_new = theta_mean + jnp.einsum(
        "pir,pij->pjr", theta - theta_mean, transform, precision=lax.Precision.HIGHEST
    )
    updated = (
        jnp.exp(theta_new)
        .astype(bf16)
        .reshape(cols, patch_rows, groups, group, reactions)
        .transpose(2, 3, 4, 1, 0)
    )
    updated = lax.all_to_all(updated, "mem", split_axis=0, concat_axis=0, tiled=True)
    mult_analysis = updated.transpose(1, 2, 0, 3, 4).reshape(
        group, reactions, groups * patch_rows, cols
    )
    return (analysis, mult_analysis)


def solution(mesh):
    return jax.shard_map(
        on_device,
        mesh=mesh,
        in_specs=(
            P("mem", None, "grid", None),
            P(None, "grid", None),
            P("mem", None, "grid", None),
            P("grid", None, None),
            P("grid", None, None),
            P("grid", None, None),
        ),
        out_specs=(P("mem", None, "grid", None), P("mem", None, "grid", None)),
        check_vma=False,
    )
```

profile of v0, /device:TPU:0, one launch (start us, length us, event | category | flops | bytes accessed | tf_op | source)
XLA Modules:
  0.0 309.3 jit_solution(8242272737259562502)
XLA Ops:
  0.6 11.3 %forward_dft.1 = bf16[8,96,2048]{2,1,0:T(8,128)(2,1)} custom-call(f32[4,4,96,1536]{3,2,1,0:T(8,128)} %x_ref.1), custom_call_target="tpu_custom_call" | custom-call | tf_op jit(solution)/shard_map/forward_dft/pallas_call | solution.py:76
  11.9 6.5 %all-to-all-start = ((bf16[8,96,2048]{2,1,0:T(8,128)(2,1)}), bf16[8,96,2048]{2,1,0:T(8,128)(2,1)S(1)}, u32[]{:S(2)}, u32[]{:S(2)}) async-start(bf16[8,96,2048]{2,1,0:T(8,128)(2,1)} %forward_dft.1), calls=%async_computation | async-start | bytes 6291456 | tf_op jit(solution)/shard_map/all_to_all | solution.py:370
  18.9 0.9 reshape.281
  19.9 6.9 %fusion.12.back_ref = bf16[768,512]{1,0:T(8,128)(2,1)} fusion(f32[512]{0:T(512)S(1)} %select_convert_fusion, f32[768]{0:T(1024)S(1)} %reshape.275, pred[]{:T(512)S(6)} %eq.80), kind=kLoop, calls=%fused_computation.19 | loop fusion | flops 1179648 | bytes 791553 | tf_op jit(solution)/shard_map/convert_element_type | solution.py:136
  26.8 6.9 %fusion.10.ahead_ref = bf16[512,768]{1,0:T(8,128)(2,1)} fusion(f32[512]{0:T(512)S(1)} %select_convert_fusion, f32[768]{0:T(1024)S(1)} %add_multiply_fusion.2, pred[]{:T(512)S(6)} %eq.80), kind=kLoop, calls=%fused_computation.17 | loop fusion | flops 1179648 | bytes 791553 | tf_op jit(solution)/shard_map/convert_element_type | solution.py:136
  33.7 56.2 %all-to-all-done = bf16[8,96,2048]{2,1,0:T(8,128)(2,1)S(1)} async-done(((bf16[8,96,2048]{2,1,0:T(8,128)(2,1)}), bf16[8,96,2048]{2,1,0:T(8,128)(2,1)S(1)}, u32[]{:S(2)}, u32[]{:S(2)}) %all-to-all-start) | async-done | bytes 3145760 | tf_op jit(solution)/shard_map/all_to_all | solution.py:370
  89.9 3.7 %all-to-all-start.2 = ((bf16[4,2,1152]{2,1,0:T(2,128)(2,1)}), bf16[4,2,1152]{2,1,0:T(2,128)(2,1)S(1)}, u32[]{:S(2)}, u32[]{:S(2)}) async-start(bf16[4,2,1152]{2,1,0:T(2,128)(2,1)} %reshape.281), calls=%async_computation.2 | async-start | bytes 36864 | tf_op jit(solution)/shard_map/all_to_all | solution.py:372
  94.5 7.3 %meridional.1 = bf16[32,4,96,128]{3,2,1,0:T(8,128)(2,1)} custom-call(bf16[768,2048]{1,0:T(8,128)(2,1)} %bitcast.139, bf16[512,768]{1,0:T(8,128)(2,1)} %fusion.10.ahead_ref, bf16[768,512]{1,0:T(8,128)(2,1)} %fusion.12.back_ref, f32[512,128]{1,0:T(8,128)} %select_multiply_fusion.gain_ref), custom_call_target="tpu_custom_call" | custom-call | tf_op jit(solution)/shard_map/meridional/pallas_call | solution.py:112
  101.8 4.2 %all-to-all-start.1 = ((bf16[32,4,96,128]{3,2,1,0:T(8,128)(2,1)}), bf16[32,4,96,128]{3,2,1,0:T(8,128)(2,1)S(1)}, u32[]{:S(2)}, u32[]{:S(2)}) async-start(bf16[32,4,96,128]{3,2,1,0:T(8,128)(2,1)} %meridional.1), calls=%async_computation.1 | async-start | bytes 6291456 | tf_op jit(solution)/shard_map/all_to_all | solution.py:414
  106.0 2.6 dynamic-slice_convert_fusion
  108.6 3.9 %reshape.276 = f32[12,8,3,1536]{3,2,1,0:T(4,128)} reshape(f32[12,24,1536]{2,1,0:T(8,128)} %dynamic-slice_convert_fusion) | data formatting | bytes 3538944 | tf_op jit(solution)/shard_map/transpose | solution.py:388
  112.6 3.5 %copy.57 = f32[12,8,3,1536]{3,1,2,0:T(8,128)} copy(f32[12,8,3,1536]{3,2,1,0:T(4,128)} %reshape.276) | data formatting | bytes 3538944 | tf_op jit(solution)/shard_map/transpose | solution.py:388
  116.1 1.1 mul.264
  117.1 2.3 mul.265
  120.0 1.3 divide_bitcast_fusion
  122.6 26.7 %fusion.5.table_ref = bf16[1024,1536]{1,0:T(8,128)(2,1)} fusion(s32[1024]{0:T(1024)S(1)} %get-tuple-element.23, s32[1024]{0:T(1024)S(1)} %get-tuple-element.22, f32[1024]{0:T(1024)S(1)} %compare_select_fusion), kind=kLoop, calls=%fused_computation.6 | loop fusion | flops 18874368 | bytes 3158016 | tf_op jit(solution)/shard_map/convert_element_type | solution.py:174
  150.5 2.6 copy.37
  154.1 24.3 %all-to-all-done.1 = bf16[32,4,96,128]{3,2,1,0:T(8,128)(2,1)S(1)} async-done(((bf16[32,4,96,128]{3,2,1,0:T(8,128)(2,1)}), bf16[32,4,96,128]{3,2,1,0:T(8,128)(2,1)S(1)}, u32[]{:S(2)}, u32[]{:S(2)}) %all-to-all-start.1) | async-done | bytes 3145760 | tf_op jit(solution)/shard_map/all_to_all | solution.py:414
  178.3 4.3 %broadcast_in_dim.38.factor_ref = f32[6,16,12,8,128]{4,3,2,1,0:T(8,128)} broadcast(f32[6,16,12,8]{3,2,1,0:T(8,128)} %copy.37), dimensions={0,1,2,3} | broadcast | bytes 4755456 | tf_op jit(solution)/shard_map/broadcast_in_dim | solution.py:390
  182.7 26.1 %chemistry.1 = (bf16[4,3,128,1536]{3,2,1,0:T(8,128)(2,1)}, f32[6,16,8,128]{3,2,1,0:T(8,128)}) custom-call(bf16[4,8,384,128]{3,2,1,0:T(8,128)(2,1)} %bitcast.138, bf16[1024,1536]{1,0:T(8,128)(2,1)} %fusion.5.table_ref, f32[12,3,8,1536]{3,2,1,0:T(8,128)} %bitcast.140, f32[6,16,12,8,128]{4,3,2,1,0:T(8,128)} %broadcast_in_dim.38.factor_ref, ...), custom_call_target="tpu_custom_call" | custom-call | tf_op jit(solution)/shard_map/chemistry/pallas_call | solution.py:260
  208.8 1.0 bitcast_reduce_fusion
  209.8 1.1 copy.38
  210.9 1.1 multiply_reduce_fusion
  222.5 1.0 fusion.19
  223.5 0.9 reshape.283
  224.4 3.5 %all-to-all-start.4 = ((bf16[4,2,1152]{2,1,0:T(2,128)(2,1)}), bf16[4,2,1152]{2,1,0:T(2,128)(2,1)S(1)}, u32[]{:S(2)}, u32[]{:S(2)}) async-start(bf16[4,2,1152]{2,1,0:T(2,128)(2,1)} %reshape.283), calls=%async_computation.4 | async-start | bytes 36864 | tf_op jit(solution)/shard_map/all_to_all | solution.py:451
  228.3 3.8 %mul.262 = f32[6,16,8,16,8]{4,3,2,1,0:T(8,128)} broadcast(f32[6,16,8,16]{3,2,1,0:T(8,128)S(1)} %copy.39), dimensions={0,1,2,3} | broadcast | bytes 442368 | tf_op jit(solution)/shard_map/mul | solution.py:426
  232.1 5.2 %mul.263 = f32[6,128,128]{2,1,0:T(8,128)S(1)} reshape(f32[6,16,8,16,8]{4,3,2,1,0:T(8,128)} %mul.262) | data formatting | bytes 786432 | tf_op jit(solution)/shard_map/mul | solution.py:426
  238.2 7.7 %apply_weights.1 = bf16[16,4,24,1536]{3,2,1,0:T(8,128)(2,1)} custom-call(bf16[6,128,128]{2,1,0:T(8,128)(2,1)} %get-tuple-element.15.high_ref, bf16[6,128,128]{2,1,0:T(8,128)(2,1)} %get-tuple-element.14.low_ref, bf16[4,3,128,1536]{3,2,1,0:T(8,128)(2,1)} %get-tuple-element.5.bg_ref), custom_call_target="tpu_custom_call" | custom-call | tf_op jit(solution)/shard_map/apply_weights/pallas_call | solution.py:311
  246.0 5.0 %all-to-all-start.3 = ((bf16[4,4,4,24,1536]{4,3,2,1,0:T(8,128)(2,1)}), bf16[4,4,4,24,1536]{4,3,2,1,0:T(8,128)(2,1)}, u32[]{:S(2)}, u32[]{:S(2)}) async-start(bf16[4,4,4,24,1536]{4,3,2,1,0:T(8,128)(2,1)} %bitcast.137), calls=%async_computation.3 | async-start | bytes 9437184 | tf_op jit(solution)/shard_map/all_to_all | solution.py:431
  252.3 51.9 %all-to-all-done.3 = bf16[4,4,4,24,1536]{4,3,2,1,0:T(8,128)(2,1)} async-done(((bf16[4,4,4,24,1536]{4,3,2,1,0:T(8,128)(2,1)}), bf16[4,4,4,24,1536]{4,3,2,1,0:T(8,128)(2,1)}, u32[]{:S(2)}, u32[]{:S(2)}) %all-to-all-start.3) | async-done | bytes 4718624 | tf_op jit(solution)/shard_map/all_to_all | solution.py:431
  304.2 5.1 %copy.40 = bf16[4,4,4,24,1536]{4,3,2,1,0:T(8,128)(2,1)} copy(bf16[4,4,4,24,1536]{4,3,1,0,2:T(8,128)(2,1)} %bitcast.26) | data formatting | bytes 9437184 | tf_op jit(solution)/shard_map/transpose | solution.py:438
  (76 shorter events, 18.5 us)
Async XLA Ops:
  11.9 6.7 %copy-start.6 = (bf16[4,12,32,6]{2,0,3,1:T(4,128)(2,1)S(1)}, bf16[4,12,32,6]{2,0,3,1:T(4,128)(2,1)}, u32[]{:S(2)}) copy-start(bf16[4,12,32,6]{2,0,3,1:T(4,128)(2,1)} %param.8) | copy-start | bytes 55300
  11.9 78.0 %all-to-all-start = ((bf16[8,96,2048]{2,1,0:T(8,128)(2,1)}), bf16[8,96,2048]{2,1,0:T(8,128)(2,1)S(1)}, u32[]{:S(2)}, u32[]{:S(2)}) async-start(bf16[8,96,2048]{2,1,0:T(8,128)(2,1)} %forward_dft.1), calls=%async_computation | async-start | bytes 6291456 | tf_op jit(solution)/shard_map/all_to_all | solution.py:370
  89.9 4.6 %copy-start.1 = (bf16[8,96,2048]{2,1,0:T(8,128)(2,1)}, bf16[8,96,2048]{2,1,0:T(8,128)(2,1)S(1)}, u32[]{:S(2)}) copy-start(bf16[8,96,2048]{2,1,0:T(8,128)(2,1)S(1)} %all-to-all-done) | copy-start | bytes 9437188
  89.9 11.9 %all-to-all-start.2 = ((bf16[4,2,1152]{2,1,0:T(2,128)(2,1)}), bf16[4,2,1152]{2,1,0:T(2,128)(2,1)S(1)}, u32[]{:S(2)}, u32[]{:S(2)}) async-start(bf16[4,2,1152]{2,1,0:T(2,128)(2,1)} %reshape.281), calls=%async_computation.2 | async-start | bytes 36864 | tf_op jit(solution)/shard_map/all_to_all | solution.py:372
  101.8 76.5 %all-to-all-start.1 = ((bf16[32,4,96,128]{3,2,1,0:T(8,128)(2,1)}), bf16[32,4,96,128]{3,2,1,0:T(8,128)(2,1)S(1)}, u32[]{:S(2)}, u32[]{:S(2)}) async-start(bf16[32,4,96,128]{3,2,1,0:T(8,128)(2,1)} %meridional.1), calls=%async_computation.1 | async-start | bytes 6291456 | tf_op jit(solution)/shard_map/all_to_all | solution.py:414
  112.6 8.8 %copy-start.7 = (s32[32,6,128]{2,0,1:T(8,128)S(1)}, s32[32,6,128]{2,0,1:T(8,128)}, u32[]{:S(2)}) copy-start(s32[32,6,128]{2,0,1:T(8,128)} %param.9) | copy-start | bytes 294916
  153.4 0.6 copy-start.4
  178.3 4.3 %copy-start = (bf16[32,4,96,128]{3,2,1,0:T(8,128)(2,1)}, bf16[32,4,96,128]{3,2,1,0:T(8,128)(2,1)S(1)}, u32[]{:S(2)}) copy-start(bf16[32,4,96,128]{3,2,1,0:T(8,128)(2,1)S(1)} %all-to-all-done.1) | copy-start | bytes 9437188
  182.7 28.2 %copy-start.3 = (f32[48,128]{1,0:T(8,128)S(1)}, f32[48,128]{1,0:T(8,128)}, u32[]{:S(2)}) copy-start(f32[48,128]{1,0:T(8,128)} %divide_bitcast_fusion) | copy-start | bytes 73732
  182.7 29.3 %copy-start.8 = (f32[16,16]{1,0:T(8,128)S(1)}, f32[16,16]{1,0:T(8,128)}, u32[]{:S(2)}) copy-start(f32[16,16]{1,0:T(8,128)} %get-tuple-element.24) | copy-start | bytes 3076
  217.3 5.1 %copy-start.5 = (f32[48,12]{1,0:T(8,128)S(1)}, f32[48,12]{1,0:T(8,128)}, u32[]{:S(2)}) copy-start(f32[48,12]{1,0:T(8,128)} %copy-done.4) | copy-start | bytes 6916
  224.4 21.6 %all-to-all-start.4 = ((bf16[4,2,1152]{2,1,0:T(2,128)(2,1)}), bf16[4,2,1152]{2,1,0:T(2,128)(2,1)S(1)}, u32[]{:S(2)}, u32[]{:S(2)}) async-start(bf16[4,2,1152]{2,1,0:T(2,128)(2,1)} %reshape.283), calls=%async_computation.4 | async-start | bytes 36864 | tf_op jit(solution)/shard_map/all_to_all | solution.py:451
  232.1 5.3 %copy-start.2 = (f32[128,128]{1,0:T(8,128)S(1)}, f32[128,128]{1,0:T(8,128)}, u32[]{:S(2)}) copy-start(f32[128,128]{1,0:T(8,128)} %mul.265) | copy-start | bytes 196612
  246.0 58.2 %all-to-all-start.3 = ((bf16[4,4,4,24,1536]{4,3,2,1,0:T(8,128)(2,1)}), bf16[4,4,4,24,1536]{4,3,2,1,0:T(8,128)(2,1)}, u32[]{:S(2)}, u32[]{:S(2)}) async-start(bf16[4,4,4,24,1536]{4,3,2,1,0:T(8,128)(2,1)} %bitcast.137), calls=%async_computation.3 | async-start | bytes 9437184 | tf_op jit(solution)/shard_map/all_to_all | solution.py:431
where the time goes:
time: 311 us; the launch traced here: 309 us
  waiting for transfers between devices  132 us (42%)
  Pallas kernels  52.4 us (17%)
  other arithmetic  51.5 us (17%)
  local copies, waits for them, and re-layouts  37.9 us (12%)
  starting transfers between devices  22.9 us (7%)
  matrix products  11.3 us (4%)
    all_to_all x1, waiting for transfers between devices, on_device(): lax.all_to_all(fourier, 'grid', split_axis=0, concat_axis=0, tiled=True)  56.2 us
    all_to_all x1, waiting for transfers between devices, on_device(): lax.all_to_all(analysed.reshape(groups, group, tracers, own, longitudes),...  51.9 us
    convert_element_type x1, other arithmetic, inverse_table(): return (weight * jnp.cos(angle)).astype(bf16)  26.7 us
    pallas_call x1, Pallas kernels, chemistry(): pl.pallas_call(chemistry_kernel, grid=(cols,), in_specs=[pl.BlockSpec(z.s...  26.1 us
    all_to_all x1, waiting for transfers between devices, on_device(): lax.all_to_all(last, ('mem', 'grid'), split_axis=0, concat_axis=0, tiled=...  24.3 us
    convert_element_type x2, other arithmetic, values(): return jnp.where(even, jnp.cos(angle), jnp.sin(angle)).astype(bf16)  13.8 us
    mul x4, local copies, waits for them, and re-layouts, on_device(): weights.transpose(0, 3, 1, 2)[..., None] * same[None, None, :, None, :]  12.4 us
    pallas_call x1, Pallas kernels, forward_transform(): pl.pallas_call(functools.partial(forward_kernel, bands, waves), grid=(gro...  11.3 us
  transfers between devices with their start and end apart: 5, of which 3 were waited for; matrix products, arithmetic and copies ran while one was open for 24% of the time, Pallas kernels for 5%

commit v1 on v0

--- a/solution.py
+++ b/solution.py
@@ -14,6 +14,8 @@
 SWEEPS = 5
 LANES = 128
 SUBLANES = 8
+CHUNKS = 2
+
 
 damping = 2.0
 f32 = jnp.float32
@@ -182,8 +184,6 @@
     members = factor_ref.shape[1]
     tracers = bg_ref.shape[0]
     others = tracers - 1
-    group = members // sources
-    own = height * patch_rows
 
     @pl.when(pl.program_id(0) == 0)
     def _():
@@ -202,7 +202,7 @@
                 rates = [
                     factor_ref[0, e, r] * rate_ref[r, i, :, lanes] for r in range(reactions)
                 ]
-                moved, kept = [], []
+                kept = []
                 for a in range(tracers):
                     outflow = rates[others * a]
                     for s in range(1, others):
@@ -252,28 +252,28 @@
     lax.fori_loop(0, members, observe, 0)
 
 
-def chemistry(z, table, rate, factor, lane, place, tracers):
+def chemistry(z, table, rate, factor, lane, place, tracers, base, cols):
     sources, bands, rows, local = z.shape
-    reactions, height, patch_rows, longitudes = rate.shape
-    cols, members = factor.shape[:2]
+    reactions, height, patch_rows, _ = rate.shape
+    members = factor.shape[1]
     observations = lane.shape[-1]
     return pl.pallas_call(
         chemistry_kernel,
         grid=(cols,),
         in_specs=[
             pl.BlockSpec(z.shape, lambda c: (0, 0, 0, 0)),
-            pl.BlockSpec((table.shape[0], PLON), lambda c: (0, c)),
-            pl.BlockSpec((reactions, height, patch_rows, PLON), lambda c: (0, 0, 0, c)),
-            pl.BlockSpec((1, members, reactions, patch_rows, LANES), lambda c: (c, 0, 0, 0, 0)),
-            pl.BlockSpec((1, patch_rows, observations), lambda c: (c, 0, 0)),
-            pl.BlockSpec((1, patch_rows, observations), lambda c: (c, 0, 0)),
+            pl.BlockSpec((table.shape[0], PLON), lambda c: (0, c + base)),
+            pl.BlockSpec((reactions, height, patch_rows, PLON), lambda c: (0, 0, 0, c + base)),
+            pl.BlockSpec((1, members, reactions, patch_rows, LANES), lambda c: (c + base, 0, 0, 0, 0)),
+            pl.BlockSpec((1, patch_rows, observations), lambda c: (c + base, 0, 0)),
+            pl.BlockSpec((1, patch_rows, observations), lambda c: (c + base, 0, 0)),
         ],
         out_specs=[
             pl.BlockSpec((tracers, height, members * patch_rows, PLON), lambda c: (0, 0, 0, c)),
             pl.BlockSpec((1, members, patch_rows, observations), lambda c: (c, 0, 0, 0)),
         ],
         out_shape=[
-            jax.ShapeDtypeStruct((tracers, height, members * patch_rows, longitudes), bf16),
+            jax.ShapeDtypeStruct((tracers, height, members * patch_rows, cols * PLON), bf16),
             jax.ShapeDtypeStruct((cols, members, patch_rows, observations), f32),
         ],
         scratch_shapes=[
@@ -282,68 +282,215 @@
             pltpu.VMEM((tracers, height, members, patch_rows, PLON), f32),
         ],
         compiler_params=pltpu.CompilerParams(vmem_limit_bytes=60 * 2**20),
+        cost_estimate=pl.CostEstimate(
+            flops=2 * sources * rows * bands * local * cols * PLON,
+            bytes_accessed=2 * math.prod(z.shape) * 8,
+            transcendentals=0,
+        ),
         name="chemistry",
     )(z, table, rate, factor, lane, place)
 
 
-def apply_kernel(high_ref, low_ref, bg_ref, o_ref, rows):
-    members, tracers, own, _ = o_ref.shape
-    height = bg_ref.shape[1]
-    patch_rows = own // height
+def precise_dot(a, b):
+    return jnp.dot(a, b, preferred_element_type=f32, precision=lax.Precision.HIGHEST)
+
+
+def member_weights(seen, measured, variance, members, patch_rows):
+    wide = members * patch_rows
+    row = lax.broadcasted_iota(jnp.int32, (wide, wide), 0)
+    column = lax.broadcasted_iota(jnp.int32, (wide, wide), 1)
+    mask = (row % patch_rows == column % patch_rows).astype(f32)
+    identity = (row == column).astype(f32)
+    spare = members - 1.0
+
+    def over_members(array):
+        return jnp.sum(array.reshape(members, patch_rows, array.shape[-1]), axis=0)
+
+    def each_member(array):
+        return jnp.concatenate([array] * members, axis=0)
+
+    currents, scales, projections = [], [], []
+    for predicted, observed, errors in zip(seen, measured, variance):
+        mean = over_members(predicted) * (1.0 / members)
+        spread = predicted - each_member(mean)
+        weighted = spread * each_member(1.0 / errors)
+        outer = mask * lax.dot_general(
+            weighted,
+            spread,
+            (((1,), (1,)), ((), ())),
+            preferred_element_type=f32,
+            precision=lax.Precision.HIGHEST,
+        )
+        square = over_members(jnp.sum(outer * outer, axis=1, keepdims=True))
+        scale = each_member(spare + jnp.sqrt(square))
+        currents.append((spare * identity + outer) * (1.0 / scale))
+        scales.append(scale)
+        innovation = each_member(observed - mean)
+        projections.append(jnp.sum(weighted * innovation, axis=1, keepdims=True))
+
+    roots = [1.5 * identity - 0.5 * current for current in currents]
+    currents = [precise_dot(c, m) for c, m in zip(currents, roots)]
+    for sweep in range(1, SWEEPS):
+        middles = [
+            1.5 * identity - 0.5 * precise_dot(r, c) for r, c in zip(roots, currents)
+        ]
+        if sweep < SWEEPS - 1:
+            currents = [precise_dot(c, m) for c, m in zip(currents, middles)]
+        roots = [precise_dot(m, r) for m, r in zip(middles, roots)]
+
+    weights = []
+    for root, scale, projected in zip(roots, scales, projections):
+        along = jnp.sum(identity * projected, axis=0, keepdims=True)
+        once = jnp.sum(root * along, axis=1, keepdims=True)
+        twice = jnp.sum(root * (once * (1.0 / scale)), axis=0, keepdims=True)
+        transform = jnp.sqrt(spare / scale) * root + mask * twice
+        rest = (1.0 - jnp.sum(transform, axis=1, keepdims=True)) * (1.0 / members)
+        weights.append(transform + mask * rest)
+    return weights
+
+
+def analysis_kernel(groups, me_ref, seen_ref, measured_ref, variance_ref, theta_ref, bg_ref, *refs):
+    outs, factors = refs[:groups], refs[groups : 2 * groups]
+    high, low, rows = refs[2 * groups :]
+    cols, patch_rows, _ = measured_ref.shape
+    group, tracers, own, _ = outs[0].shape
+    members = groups * group
+    height = own // patch_rows
+    block = group * patch_rows
+    at = pl.program_id(0)
+
+    @pl.when(at == 0)
+    def _():
+        weights = member_weights(
+            [seen_ref[c] for c in range(cols)],
+            [measured_ref[c] for c in range(cols)],
+            [variance_ref[c] for c in range(cols)],
+            members,
+            patch_rows,
+        )
+        for c in range(cols):
+            upper = weights[c].astype(bf16)
+            high[c] = weights[c]
+            low[c] = weights[c] - upper.astype(f32)
+
+    def by_partner(ref):
+        parts = []
+        for j in range(groups):
+            start = pl.multiple_of((me_ref[0] ^ j) * block, block)
+            parts.append(ref[at, pl.ds(start, block), :])
+        return jnp.concatenate(parts, axis=0)
+
+    exact = by_partner(high)
+    updated = jnp.exp(precise_dot(exact, theta_ref[0])).astype(bf16)
+    for j in range(groups):
+        factors[j][0] = updated[j * block : (j + 1) * block]
+    upper = exact.astype(bf16)
+    lower = by_partner(low).astype(bf16)
     for t in range(tracers):
         for i in range(height):
             value = bg_ref[t, i]
-            new = jnp.dot(high_ref[0], value, preferred_element_type=f32)
-            new = new + jnp.dot(low_ref[0], value, preferred_element_type=f32)
-            for j in range(members):
-                part = new[j * patch_rows : (j + 1) * patch_rows]
+            new = jnp.dot(upper, value, preferred_element_type=f32)
+            new = new + jnp.dot(lower, value, preferred_element_type=f32)
+            for e in range(members):
+                part = new[e * patch_rows : (e + 1) * patch_rows]
                 for k in range(PLON // LANES):
-                    rows[k, j, pl.ds(i, patch_rows, stride=height), :] = part[
+                    rows[k, e, pl.ds(i, patch_rows, stride=height), :] = part[
                         :, k * LANES : (k + 1) * LANES
                     ]
-        for k in range(PLON // LANES):
-            o_ref[:, t, :, k * LANES : (k + 1) * LANES] = rows[k].astype(bf16)
-
-
-def apply_weights(high, low, bg, members, own):
+        for j in range(groups):
+            for k in range(PLON // LANES):
+                outs[j][:, t, :, k * LANES : (k + 1) * LANES] = rows[
+                    k, j * group : (j + 1) * group
+                ].astype(bf16)
+
+
+def analyse(me, seen, measured, variance, theta, bg, base, groups, own):
+    cols, members, patch_rows, observations = seen.shape
+    group = members // groups
     tracers, height, wide, longitudes = bg.shape
-    cols = high.shape[0]
+    block = group * patch_rows
+    lanes = theta.shape[-1]
+    whole = lambda c, me: (0, 0, 0)
+    shifted = lambda c, me: (base // cols, 0, 0)
     return pl.pallas_call(
-        apply_kernel,
-        grid=(cols,),
-        in_specs=[
-            pl.BlockSpec((1, wide, wide), lambda c: (c, 0, 0)),
-            pl.BlockSpec((1, wide, wide), lambda c: (c, 0, 0)),
-            pl.BlockSpec((tracers, height, wide, PLON), lambda c: (0, 0, 0, c)),
-        ],
-        out_specs=pl.BlockSpec((members, tracers, own, PLON), lambda c: (0, 0, 0, c)),
-        out_shape=jax.ShapeDtypeStruct((members, tracers, own, longitudes), bf16),
-        scratch_shapes=[pltpu.VMEM((PLON // LANES, members, own, LANES), f32)],
+        functools.partial(analysis_kernel, groups),
+        grid_spec=pltpu.PrefetchScalarGridSpec(
+            num_scalar_prefetch=1,
+            grid=(cols,),
+            in_specs=[
+                pl.BlockSpec((cols, wide, observations), whole),
+                pl.BlockSpec((cols, patch_rows, observations), shifted),
+                pl.BlockSpec((cols, patch_rows, observations), shifted),
+                pl.BlockSpec((1, wide, lanes), lambda c, me: (c + base, 0, 0)),
+                pl.BlockSpec((tracers, height, wide, PLON), lambda c, me: (0, 0, 0, c)),
+            ],
+            out_specs=[pl.BlockSpec((group, tracers, own, PLON), lambda c, me: (0, 0, 0, c))]
+            * groups
+            + [pl.BlockSpec((1, block, lanes), lambda c, me: (c, 0, 0))] * groups,
+            scratch_shapes=[
+                pltpu.VMEM((cols, wide, wide), f32),
+                pltpu.VMEM((cols, wide, wide), f32),
+                pltpu.VMEM((PLON // LANES, members, own, LANES), f32),
+            ],
+        ),
+        out_shape=[jax.ShapeDtypeStruct((group, tracers, own, longitudes), bf16)] * groups
+        + [jax.ShapeDtypeStruct((cols, block, lanes), bf16)] * groups,
         compiler_params=pltpu.CompilerParams(vmem_limit_bytes=60 * 2**20),
-        name="apply_weights",
-    )(high, low, bg)
-
-
-def ensemble_transform(predicted, observed, variance):
-    highest = lax.Precision.HIGHEST
-    members = predicted.shape[1]
-    seen_mean = jnp.mean(predicted, axis=1, keepdims=True)
-    seen_spread = predicted - seen_mean
-    weighted = seen_spread * (1.0 / variance)[:, None, :]
-    outer = jnp.einsum("pik,pjk->pij", weighted, seen_spread, precision=highest)
-    scale = members - 1.0 + jnp.sqrt(jnp.sum(outer * outer, axis=(1, 2)))
-    identity = jnp.eye(members, dtype=f32)
-    current = ((members - 1.0) * identity + outer) / scale[:, None, None]
-    root = jnp.broadcast_to(identity, current.shape)
-    for sweep in range(SWEEPS):
-        middle = 1.5 * identity - 0.5 * jnp.einsum("pij,pjk->pik", root, current, precision=highest)
-        current = jnp.einsum("pij,pjk->pik", current, middle, precision=highest)
-        root = jnp.einsum("pij,pjk->pik", middle, root, precision=highest)
-    covariance = jnp.einsum("pij,pjk->pik", root, root, precision=highest) / scale[:, None, None]
-    innovation = observed - seen_mean[:, 0, :]
-    projected = jnp.einsum("pjk,pk->pj", weighted, innovation, precision=highest)
-    coefficient = jnp.einsum("pij,pj->pi", covariance, projected, precision=highest)
-    return jnp.sqrt((members - 1.0) / scale)[:, None, None] * root + coefficient[:, :, None]
+        cost_estimate=pl.CostEstimate(
+            flops=6 * 10**9, bytes_accessed=8 * tracers * height * wide * longitudes, transcendentals=0
+        ),
+        name="analysis",
+    )(me, seen.reshape(cols, wide, observations), measured, variance, theta, bg)
+
+
+def assemble_kernel(groups, first, lanes, me_ref, *refs):
+    pieces = refs[:groups]
+    out = refs[groups + (0 if first else 1)]
+    buffer, arrived, left = refs[-3:]
+    own = pieces[0].shape[2]
+    ins, outs = [], []
+    for j in range(groups):
+        ins.append(pltpu.make_async_copy(pieces[j], buffer.at[j], arrived.at[j]))
+        ins[j].start()
+    for j in range(groups):
+        start = pl.multiple_of((me_ref[0] ^ j) * own, own)
+        ins[j].wait()
+        outs.append(
+            pltpu.make_async_copy(
+                buffer.at[j], out.at[:, :, pl.ds(start, own), lanes], left.at[j]
+            )
+        )
+        outs[j].start()
+    for j in range(groups):
+        outs[j].wait()
+
+
+def assemble(me, pieces, before, start, shape):
+    groups = len(pieces)
+    width = pieces[0].shape[-1]
+    any_spec = pl.BlockSpec(memory_space=pl.ANY)
+    extra = [] if before is None else [before]
+    return pl.pallas_call(
+        functools.partial(assemble_kernel, groups, before is None, pl.ds(start, width)),
+        grid_spec=pltpu.PrefetchScalarGridSpec(
+            num_scalar_prefetch=1,
+            grid=(1,),
+            in_specs=[any_spec] * (groups + len(extra)),
+            out_specs=any_spec,
+            scratch_shapes=[
+                pltpu.VMEM((groups,) + pieces[0].shape, bf16),
+                pltpu.SemaphoreType.DMA((groups,)),
+                pltpu.SemaphoreType.DMA((groups,)),
+            ],
+        ),
+        out_shape=jax.ShapeDtypeStruct(shape, bf16),
+        input_output_aliases={} if before is None else {groups + 1: 0},
+        compiler_params=pltpu.CompilerParams(vmem_limit_bytes=40 * 2**20),
+        cost_estimate=pl.CostEstimate(
+            flops=0, bytes_accessed=2 * 2 * groups * math.prod(pieces[0].shape), transcendentals=0
+        ),
+        name="assemble",
+    )(me, *pieces, *extra)
 
 
 def on_device(
@@ -413,45 +560,47 @@
     )
     returned = lax.all_to_all(last, ("mem", "grid"), split_axis=0, concat_axis=0, tiled=True)
     z = returned.reshape(groups, bands, group * tracers * own, 2 * waves)
-    bg, seen = chemistry(z, inverse, rate, factor, lane, place, tracers)
-
-    patches = cols * patch_rows
-    predicted = seen.transpose(0, 2, 1, 3).reshape(patches, members, -1)
-    transform = ensemble_transform(
-        predicted, observed.reshape(patches, -1), variance.reshape(patches, -1)
-    )
-    weights = transform + (1.0 - jnp.sum(transform, axis=1, keepdims=True)) / members
-    weights = weights.reshape(cols, patch_rows, members, members)
-    same = jnp.eye(patch_rows, dtype=f32)
-    spread = weights.transpose(0, 3, 1, 2)[..., None] * same[None, None, :, None, :]
-    spread = spread.reshape(cols, members * patch_rows, members * patch_rows)
-    high = spread.astype(bf16)
-    low = (spread - high.astype(f32)).astype(bf16)
-    analysed = apply_weights(high, low, bg, members, own)
-    landed = lax.all_to_all(
-        analysed.reshape(groups, group, tracers, own, longitudes),
-        "mem",
-        split_axis=0,
-        concat_axis=0,
-        tiled=True,
-    )
-    analysis = landed.transpose(1, 2, 0, 3, 4).reshape(group, tracers, band, longitudes)
-
-    theta = jnp.log(factors.astype(f32)).transpose(3, 2, 0, 1).reshape(patches, members, reactions)
-    theta_mean = jnp.mean(theta, axis=1, keepdims=True)
-    theta_new = theta_mean + jnp.einsum(
-        "pir,pij->pjr", theta - theta_mean, transform, precision=lax.Precision.HIGHEST
-    )
-    updated = (
-        jnp.exp(theta_new)
-        .astype(bf16)
-        .reshape(cols, patch_rows, groups, group, reactions)
-        .transpose(2, 3, 4, 1, 0)
-    )
-    updated = lax.all_to_all(updated, "mem", split_axis=0, concat_axis=0, tiled=True)
-    mult_analysis = updated.transpose(1, 2, 0, 3, 4).reshape(
-        group, reactions, groups * patch_rows, cols
-    )
+    me = mem.astype(jnp.int32).reshape(1)
+    theta = jnp.pad(
+        jnp.log(factors.astype(f32)).transpose(3, 0, 2, 1),
+        ((0, 0), (0, 0), (0, 0), (0, LANES - reactions)),
+    ).reshape(cols, members * patch_rows, LANES)
+
+    chunks = CHUNKS if cols % CHUNKS == 0 else 1
+    per = cols // chunks
+    landed, updated = [], []
+    for chunk in range(chunks):
+        base = chunk * per
+        bg, seen = chemistry(z, inverse, rate, factor, lane, place, tracers, base, per)
+        results = analyse(me, seen, observed, variance, theta, bg, base, groups, own)
+        if chunk < chunks - 1:
+            z, results = lax.optimization_barrier((z, results))
+        sent = []
+        for j, result in enumerate(results):
+            pairs = [(i, i ^ (j % groups)) for i in range(groups)]
+            sent.append(result if j % groups == 0 else lax.ppermute(result, "mem", pairs))
+        landed.append(sent[:groups])
+        updated.append(sent[groups:])
+
+    shape = (group, tracers, band, longitudes)
+    order = mem ^ jnp.arange(groups, dtype=jnp.int32)
+    if own % SUBLANES == 0:
+        analysis = None
+        for chunk in range(chunks):
+            analysis = assemble(me, landed[chunk], analysis, chunk * per * PLON, shape)
+    else:
+        joined = jnp.stack(
+            [jnp.concatenate([part[j] for part in landed], axis=-1) for j in range(groups)]
+        )
+        joined = jnp.take(joined, order, axis=0)
+        analysis = joined.transpose(1, 2, 0, 3, 4).reshape(shape)
+    fresh = jnp.stack([jnp.concatenate([part[j] for part in updated]) for j in range(groups)])
+    fresh = fresh[..., :reactions].reshape(groups, cols, group, patch_rows, reactions)
+    mine = (order[:, None] == jnp.arange(groups, dtype=jnp.int32)[None, :]).astype(bf16)
+    mult_analysis = jnp.einsum(
+        "jr,jcgpa->garpc", mine, fresh, preferred_element_type=f32
+    ).astype(bf16)
+    mult_analysis = mult_analysis.reshape(group, reactions, groups * patch_rows, cols)
     return (analysis, mult_analysis)
 
 

time: 311 us -> 298 us (0.958)
  Pallas kernels: 52.4 us -> 71.1 us
  local copies, waits for them, and re-layouts: 37.9 us -> 19.9 us
  matrix products: 11.3 us -> 0.24 us
  starting transfers between devices: 22.9 us -> 27.1 us
  other arithmetic: 51.5 us -> 47.8 us
    all_to_all x2 -> x0, waiting for transfers between devices: 51.9 us -> none  [the longest x1 51.9 us: on_device(): lax.all_to_all(analysed.reshape(groups, group, tracers, own, longitudes),...]
    ppermute x0 -> x12, waiting for transfers between devices: none -> 44.6 us  [on_device(): lax.ppermute(result, 'mem', pairs)]
    pallas_call x1 -> x4, Pallas kernels: 7.74 us -> 22 us  [the longest x2 17.4 us: analyse(): pl.pallas_call(functools.partial(analysis_kernel, groups), grid_spec=pltp...]
    ppermute x0 -> x12, starting transfers between devices: none -> 12.7 us  [on_device(): lax.ppermute(result, 'mem', pairs)]
    mul x4 -> x0, local copies, waits for them, and re-layouts: 12.4 us -> none  [on_device(): weights.transpose(0, 3, 1, 2)[..., None] * same[None, None, :, None, :]]
    dot_general x19 -> x1, matrix products: 11.3 us -> 0.24 us  [on_device(): jnp.einsum('jr,jcgpa->garpc', mine, fresh, preferred_element_type=f32)]
    all_to_all x2 -> x0, starting transfers between devices: 8.47 us -> none  [the longest x1 4.96 us: on_device(): lax.all_to_all(analysed.reshape(groups, group, tracers, own, longitudes),...]
    transpose x4 -> x1, local copies, waits for them, and re-layouts: 6.51 us -> 1.36 us  [own_patches(): return mine.transpose(1, 0, 2)]
  transfers between devices with their start and end apart: 5 -> 15, of which waited for: 3 -> 5; matrix products, arithmetic and copies ran while one was open for 24% -> 21% of each run, Pallas kernels for 5% -> 6%
where the time goes in v1:
time: 298 us; the launch traced here: 296 us
  waiting for transfers between devices  129 us (43%)
  Pallas kernels  71.1 us (24%)
  other arithmetic  47.8 us (16%)
  starting transfers between devices  27.1 us (9%)
  local copies, waits for them, and re-layouts  19.9 us (7%)
    all_to_all x1, waiting for transfers between devices, on_device(): lax.all_to_all(fourier, 'grid', split_axis=0, concat_axis=0, tiled=True)  56.2 us
    ppermute x12, waiting for transfers between devices, on_device(): lax.ppermute(result, 'mem', pairs)  44.6 us
    pallas_call x2, Pallas kernels, chemistry(): pl.pallas_call(chemistry_kernel, grid=(cols,), in_specs=[pl.BlockSpec(z.s...  30.6 us
    all_to_all x1, waiting for transfers between devices, on_device(): lax.all_to_all(last, ('mem', 'grid'), split_axis=0, concat_axis=0, tiled=...  28.4 us
    convert_element_type x1, other arithmetic, inverse_table(): return (weight * jnp.cos(angle)).astype(bf16)  26.7 us
    pallas_call x2, Pallas kernels, analyse(): pl.pallas_call(functools.partial(analysis_kernel, groups), grid_spec=pltp...  17.4 us
    convert_element_type x2, other arithmetic, values(): return jnp.where(even, jnp.cos(angle), jnp.sin(angle)).astype(bf16)  13.8 us
    ppermute x12, starting transfers between devices, on_device(): lax.ppermute(result, 'mem', pairs)  12.7 us
  transfers between devices with their start and end apart: 15, of which 5 were waited for; matrix products, arithmetic and copies ran while one was open for 21% of the time, Pallas kernels for 6%

profile of v1, /device:TPU:0, one launch (start us, length us, event | category | flops | bytes accessed | tf_op | source)
XLA Modules:
  0.0 296.5 jit_solution(115500946622983738)
XLA Ops:
  0.6 11.3 %forward_dft.1 = bf16[8,96,2048]{2,1,0:T(8,128)(2,1)} custom-call(f32[4,4,96,1536]{3,2,1,0:T(8,128)} %x_ref.1), custom_call_target="tpu_custom_call" | custom-call | tf_op jit(solution)/shard_map/forward_dft/pallas_call | solution.py:78
  11.9 6.5 %all-to-all-start = ((bf16[8,96,2048]{2,1,0:T(8,128)(2,1)}), bf16[8,96,2048]{2,1,0:T(8,128)(2,1)S(1)}, u32[]{:S(2)}, u32[]{:S(2)}) async-start(bf16[8,96,2048]{2,1,0:T(8,128)(2,1)} %forward_dft.1), calls=%async_computation | async-start | bytes 6291456 | tf_op jit(solution)/shard_map/all_to_all | solution.py:517
  19.9 6.9 %fusion.12.back_ref = bf16[768,512]{1,0:T(8,128)(2,1)} fusion(f32[512]{0:T(512)S(1)} %select_convert_fusion, f32[768]{0:T(1024)S(1)} %reshape.203, pred[]{:T(512)S(6)} %eq.66), kind=kLoop, calls=%fused_computation.19 | loop fusion | flops 1179648 | bytes 791553 | tf_op jit(solution)/shard_map/convert_element_type | solution.py:138
  26.8 6.9 %fusion.10.ahead_ref = bf16[512,768]{1,0:T(8,128)(2,1)} fusion(f32[512]{0:T(512)S(1)} %select_convert_fusion, f32[768]{0:T(1024)S(1)} %add_multiply_fusion.2, pred[]{:T(512)S(6)} %eq.66), kind=kLoop, calls=%fused_computation.17 | loop fusion | flops 1179648 | bytes 791553 | tf_op jit(solution)/shard_map/convert_element_type | solution.py:138
  33.7 56.2 %all-to-all-done = bf16[8,96,2048]{2,1,0:T(8,128)(2,1)S(1)} async-done(((bf16[8,96,2048]{2,1,0:T(8,128)(2,1)}), bf16[8,96,2048]{2,1,0:T(8,128)(2,1)S(1)}, u32[]{:S(2)}, u32[]{:S(2)}) %all-to-all-start) | async-done | bytes 3145760 | tf_op jit(solution)/shard_map/all_to_all | solution.py:517
  89.9 3.7 %all-to-all-start.2 = ((bf16[4,2,1152]{2,1,0:T(2,128)(2,1)}), bf16[4,2,1152]{2,1,0:T(2,128)(2,1)S(1)}, u32[]{:S(2)}, u32[]{:S(2)}) async-start(bf16[4,2,1152]{2,1,0:T(2,128)(2,1)} %reshape.206), calls=%async_computation.2 | async-start | bytes 36864 | tf_op jit(solution)/shard_map/all_to_all | solution.py:519
  94.5 7.3 %meridional.1 = bf16[32,4,96,128]{3,2,1,0:T(8,128)(2,1)} custom-call(bf16[768,2048]{1,0:T(8,128)(2,1)} %bitcast.81, bf16[512,768]{1,0:T(8,128)(2,1)} %fusion.10.ahead_ref, bf16[768,512]{1,0:T(8,128)(2,1)} %fusion.12.back_ref, f32[512,128]{1,0:T(8,128)} %select_multiply_fusion.gain_ref), custom_call_target="tpu_custom_call" | custom-call | tf_op jit(solution)/shard_map/meridional/pallas_call | solution.py:114
  101.8 4.2 %all-to-all-start.1 = ((bf16[32,4,96,128]{3,2,1,0:T(8,128)(2,1)}), bf16[32,4,96,128]{3,2,1,0:T(8,128)(2,1)S(1)}, u32[]{:S(2)}, u32[]{:S(2)}) async-start(bf16[32,4,96,128]{3,2,1,0:T(8,128)(2,1)} %meridional.1), calls=%async_computation.1 | async-start | bytes 6291456 | tf_op jit(solution)/shard_map/all_to_all | solution.py:561
  106.0 2.6 dynamic-slice_convert_fusion
  108.7 4.0 %reshape.204 = f32[12,8,3,1536]{3,2,1,0:T(4,128)} reshape(f32[12,24,1536]{2,1,0:T(8,128)} %dynamic-slice_convert_fusion) | data formatting | bytes 3538944 | tf_op jit(solution)/shard_map/transpose | solution.py:535
  112.6 3.4 %copy.43 = f32[12,8,3,1536]{3,1,2,0:T(8,128)} copy(f32[12,8,3,1536]{3,2,1,0:T(4,128)} %reshape.204) | data formatting | bytes 3538944 | tf_op jit(solution)/shard_map/transpose | solution.py:535
  116.7 1.4 dynamic-slice_bitcast_fusion
  118.7 26.7 %fusion.5.table_ref = bf16[1024,1536]{1,0:T(8,128)(2,1)} fusion(s32[1024]{0:T(1024)S(1)} %get-tuple-element.71, s32[1024]{0:T(1024)S(1)} %get-tuple-element.70, f32[1024]{0:T(1024)S(1)} %compare_select_fusion), kind=kLoop, calls=%fused_computation.6 | loop fusion | flops 18874368 | bytes 3158016 | tf_op jit(solution)/shard_map/convert_element_type | solution.py:176
  146.6 2.5 copy.29
  150.0 28.4 %all-to-all-done.1 = bf16[32,4,96,128]{3,2,1,0:T(8,128)(2,1)S(1)} async-done(((bf16[32,4,96,128]{3,2,1,0:T(8,128)(2,1)}), bf16[32,4,96,128]{3,2,1,0:T(8,128)(2,1)S(1)}, u32[]{:S(2)}, u32[]{:S(2)}) %all-to-all-start.1) | async-done | bytes 3145760 | tf_op jit(solution)/shard_map/all_to_all | solution.py:561
  178.4 4.3 %broadcast_in_dim.50.factor_ref = f32[6,16,12,8,128]{4,3,2,1,0:T(8,128)} broadcast(f32[6,16,12,8]{3,2,1,0:T(8,128)} %copy.29), dimensions={0,1,2,3} | broadcast | bytes 4755456 | tf_op jit(solution)/shard_map/broadcast_in_dim | solution.py:537
  182.7 15.3 %chemistry.2 = (bf16[4,3,128,768]{3,2,1,0:T(8,128)(2,1)}, f32[3,16,8,128]{3,2,1,0:T(8,128)}) custom-call(bf16[4,8,384,128]{3,2,1,0:T(8,128)(2,1)} %bitcast.77, bf16[1024,1536]{1,0:T(8,128)(2,1)} %fusion.5.table_ref, f32[12,3,8,1536]{3,2,1,0:T(8,128)} %bitcast.79, f32[6,16,12,8,128]{4,3,2,1,0:T(8,128)} %broadcast_in_dim.50.factor_ref, ...), custom_call_target="tpu_custom_call" | custom-call | flops 2415919104 | bytes 25165824 | tf_op jit(solution)/shard_map/chemistry/pallas_call | solution.py:260
  198.0 8.6 %analysis.2 = (bf16[4,4,24,768]{3,2,1,0:T(8,128)(2,1)}, bf16[4,4,24,768]{3,2,1,0:T(8,128)(2,1)}, bf16[4,4,24,768]{3,2,1,0:T(8,128)(2,1)}, bf16[4,4,24,768]{3,2,1...) custom-call(s32[1]{0:T(128)} %bitcast.me_ref, ...), custom_call_target="tpu_custom_call" | custom-call | flops 6000000000 | bytes 9437184 | tf_op jit(solution)/shard_map/analysis/pallas_call | solution.py:415
  206.5 15.3 %chemistry.3 = (bf16[4,3,128,768]{3,2,1,0:T(8,128)(2,1)}, f32[3,16,8,128]{3,2,1,0:T(8,128)}) custom-call(bf16[4,8,384,128]{3,2,1,0:T(8,128)(2,1)} %bitcast.78, bf16[1024,1536]{1,0:T(8,128)(2,1)} %fusion.5.table_ref, f32[12,3,8,1536]{3,2,1,0:T(8,128)} %bitcast.80, f32[6,16,12,8,128]{4,3,2,1,0:T(8,128)} %broadcast_in_dim.50.factor_ref, ...), custom_call_target="tpu_custom_call" | custom-call | flops 2415919104 | bytes 25165824 | tf_op jit(solution)/shard_map/chemistry/pallas_call | solution.py:260
  221.9 8.8 %analysis.3 = (bf16[4,4,24,768]{3,2,1,0:T(8,128)(2,1)}, bf16[4,4,24,768]{3,2,1,0:T(8,128)(2,1)}, bf16[4,4,24,768]{3,2,1,0:T(8,128)(2,1)}, bf16[4,4,24,768]{3,2,1...) custom-call(s32[1]{0:T(128)} %bitcast.me_ref, ...), custom_call_target="tpu_custom_call" | custom-call | flops 6000000000 | bytes 9437184 | tf_op jit(solution)/shard_map/analysis/pallas_call | solution.py:415
  230.7 2.1 collective-permute-start.7
  232.8 1.4 collective-permute-start.9
  234.9 3.0 %collective-permute-done.7 = bf16[3,32,128]{2,1,0:T(8,128)(2,1)S(1)} collective-permute-done((bf16[3,32,128]{2,1,0:T(8,128)(2,1)}, bf16[3,32,128]{2,1,0:T(8,128)(2,1)S(1)}, u32[]{:S(2)}, u32[]{:S(2)}) %collective-permute-start.7) | collective-permute-done | bytes 24608 | tf_op jit(solution)/shard_map/ppermute | solution.py:581
  237.8 1.6 collective-permute-start.11
  239.4 1.4 collective-permute-start.10
  241.5 1.3 collective-permute-start.4
  243.7 1.4 collective-permute-start
  248.2 1.8 copy.33
  250.0 22.8 %collective-permute-done.4.refs_2_ = bf16[4,4,24,768]{3,2,1,0:T(8,128)(2,1)S(1)} collective-permute-done((bf16[4,4,24,768]{3,2,1,0:T(8,128)(2,1)}, bf16[4,4,24,768]{3,2,1,0:T(8,128)(2,1)S(1)}, u32[]{:S(2)}, u32[]{:S(2)}) %collective-permute-start.4) | collective-permute-done | bytes 589856 | tf_op jit(solution)/shard_map/ppermute | solution.py:581
  272.8 2.0 assemble.2.refs_4_
  274.8 18.8 %collective-permute-done.1.refs_2_ = bf16[4,4,24,768]{3,2,1,0:T(8,128)(2,1)S(1)} collective-permute-done((bf16[4,4,24,768]{3,2,1,0:T(8,128)(2,1)}, bf16[4,4,24,768]{3,2,1,0:T(8,128)(2,1)S(1)}, u32[]{:S(2)}, u32[]{:S(2)}) %collective-permute-start.1) | collective-permute-done | bytes 589856 | tf_op jit(solution)/shard_map/ppermute | solution.py:581
  293.6 2.7 assemble.3
  (64 shorter events, 11.1 us)
Async XLA Ops:
  11.9 6.7 %copy-start.4 = (bf16[4,12,32,6]{2,0,3,1:T(4,128)(2,1)S(1)}, bf16[4,12,32,6]{2,0,3,1:T(4,128)(2,1)}, u32[]{:S(2)}) copy-start(bf16[4,12,32,6]{2,0,3,1:T(4,128)(2,1)} %param.8) | copy-start | bytes 55300
  11.9 78.0 %all-to-all-start = ((bf16[8,96,2048]{2,1,0:T(8,128)(2,1)}), bf16[8,96,2048]{2,1,0:T(8,128)(2,1)S(1)}, u32[]{:S(2)}, u32[]{:S(2)}) async-start(bf16[8,96,2048]{2,1,0:T(8,128)(2,1)} %forward_dft.1), calls=%async_computation | async-start | bytes 6291456 | tf_op jit(solution)/shard_map/all_to_all | solution.py:517
  89.9 4.6 %copy-start.3 = (bf16[8,96,2048]{2,1,0:T(8,128)(2,1)}, bf16[8,96,2048]{2,1,0:T(8,128)(2,1)S(1)}, u32[]{:S(2)}) copy-start(bf16[8,96,2048]{2,1,0:T(8,128)(2,1)S(1)} %all-to-all-done) | copy-start | bytes 9437188
  89.9 11.9 %all-to-all-start.2 = ((bf16[4,2,1152]{2,1,0:T(2,128)(2,1)}), bf16[4,2,1152]{2,1,0:T(2,128)(2,1)S(1)}, u32[]{:S(2)}, u32[]{:S(2)}) async-start(bf16[4,2,1152]{2,1,0:T(2,128)(2,1)} %reshape.206), calls=%async_computation.2 | async-start | bytes 36864 | tf_op jit(solution)/shard_map/all_to_all | solution.py:519
  101.8 76.5 %all-to-all-start.1 = ((bf16[32,4,96,128]{3,2,1,0:T(8,128)(2,1)}), bf16[32,4,96,128]{3,2,1,0:T(8,128)(2,1)S(1)}, u32[]{:S(2)}, u32[]{:S(2)}) async-start(bf16[32,4,96,128]{3,2,1,0:T(8,128)(2,1)} %meridional.1), calls=%async_computation.1 | async-start | bytes 6291456 | tf_op jit(solution)/shard_map/all_to_all | solution.py:561
  108.6 7.4 %copy-start.5 = (s32[32,6,128]{2,0,1:T(8,128)S(1)}, s32[32,6,128]{2,0,1:T(8,128)}, u32[]{:S(2)}) copy-start(s32[32,6,128]{2,0,1:T(8,128)} %param.9) | copy-start | bytes 294916
  178.4 4.3 %copy-start.2 = (bf16[32,4,96,128]{3,2,1,0:T(8,128)(2,1)}, bf16[32,4,96,128]{3,2,1,0:T(8,128)(2,1)S(1)}, u32[]{:S(2)}) copy-start(bf16[32,4,96,128]{3,2,1,0:T(8,128)(2,1)S(1)} %all-to-all-done.1) | copy-start | bytes 9437188
  221.8 24.4 %collective-permute-start.3 = (bf16[4,4,24,768]{3,2,1,0:T(8,128)(2,1)}, bf16[4,4,24,768]{3,2,1,0:T(8,128)(2,1)S(1)}, u32[]{:S(2)}, u32[]{:S(2)}) collective-permute-start(bf16[4,4,24,768]{3,2,1,0:T(8,128)(2,1)} %get-tuple-element.49), channel_id=1, source_target_pairs={{0,8},{8,0},{16,24},{24,16},{1,9},{9,1},{17,25},{25,17},{2,10},{10... | collective-permute-start | bytes 1769480 | tf_op jit(solution)/shard_map/ppermute | solution.py:581
  221.8 10.9 %copy-start.9 = (bf16[3,32,128]{2,1,0:T(8,128)(2,1)S(1)}, bf16[3,32,128]{2,1,0:T(8,128)(2,1)}, u32[]{:S(2)}) copy-start(bf16[3,32,128]{2,1,0:T(8,128)(2,1)} %get-tuple-element.54) | copy-start | bytes 73732
  221.9 12.4 %copy-start.8 = (bf16[3,32,128]{2,1,0:T(8,128)(2,1)S(1)}, bf16[3,32,128]{2,1,0:T(8,128)(2,1)}, u32[]{:S(2)}) copy-start(bf16[3,32,128]{2,1,0:T(8,128)(2,1)} %get-tuple-element.56) | copy-start | bytes 73732
  221.9 17.5 %copy-start.7 = (bf16[3,32,128]{2,1,0:T(8,128)(2,1)S(1)}, bf16[3,32,128]{2,1,0:T(8,128)(2,1)}, u32[]{:S(2)}) copy-start(bf16[3,32,128]{2,1,0:T(8,128)(2,1)} %get-tuple-element.58) | copy-start | bytes 73732
  221.9 18.9 %copy-start.6 = (bf16[3,32,128]{2,1,0:T(8,128)(2,1)S(1)}, bf16[3,32,128]{2,1,0:T(8,128)(2,1)}, u32[]{:S(2)}) copy-start(bf16[3,32,128]{2,1,0:T(8,128)(2,1)} %get-tuple-element.52) | copy-start | bytes 73732
  221.9 50.9 %copy-start = (bf16[4,4,24,768]{3,2,1,0:T(8,128)(2,1)S(1)}, bf16[4,4,24,768]{3,2,1,0:T(8,128)(2,1)}, u32[]{:S(2)}) copy-start(bf16[4,4,24,768]{3,2,1,0:T(8,128)(2,1)} %get-tuple-element.48.refs_0_) | copy-start | bytes 1769476
  230.7 7.2 %collective-permute-start.7 = (bf16[3,32,128]{2,1,0:T(8,128)(2,1)}, bf16[3,32,128]{2,1,0:T(8,128)(2,1)S(1)}, u32[]{:S(2)}, u32[]{:S(2)}) collective-permute-start(bf16[3,32,128]{2,1,0:T(8,128)(2,1)} %get-tuple-element.55), channel_id=1, source_target_pairs={{0,8},{8,0},{16,24},{24,16},{1,9},{9,1},{17,25},{25,17},{2,10},{10... | collective-permute-start | bytes 73736 | tf_op jit(solution)/shard_map/ppermute | solution.py:581
  232.7 6.6 %collective-permute-start.6 = (bf16[3,32,128]{2,1,0:T(8,128)(2,1)S(1)}, bf16[3,32,128]{2,1,0:T(8,128)(2,1)S(1)}, u32[]{:S(2)}, u32[]{:S(2)}) collective-permute-start(bf16[3,32,128]{2,1,0:T(8,128)(2,1)S(1)} %copy-done.9), channel_id=1, source_target_pairs={{0,8},{8,0},{16,24},{24,16},{1,9},{9,1},{17,25},{25,17},{2,10},{10... | collective-permute-start | bytes 73736 | tf_op jit(solution)/shard_map/ppermute | solution.py:581
  232.8 8.7 %collective-permute-start.9 = (bf16[3,32,128]{2,1,0:T(8,128)(2,1)}, bf16[3,32,128]{2,1,0:T(8,128)(2,1)S(1)}, u32[]{:S(2)}, u32[]{:S(2)}) collective-permute-start(bf16[3,32,128]{2,1,0:T(8,128)(2,1)} %get-tuple-element.57), channel_id=1, source_target_pairs={{0,16},{8,24},{16,0},{24,8},{1,17},{9,25},{17,1},{25,9},{2,18},{10... | collective-permute-start | bytes 73736 | tf_op jit(solution)/shard_map/ppermute | solution.py:581
  234.2 8.5 %collective-permute-start.8 = (bf16[3,32,128]{2,1,0:T(8,128)(2,1)S(1)}, bf16[3,32,128]{2,1,0:T(8,128)(2,1)S(1)}, u32[]{:S(2)}, u32[]{:S(2)}) collective-permute-start(bf16[3,32,128]{2,1,0:T(8,128)(2,1)S(1)} %copy-done.8), channel_id=1, source_target_pairs={{0,16},{8,24},{16,0},{24,8},{1,17},{9,25},{17,1},{25,9},{2,18},{10... | collective-permute-start | bytes 73736 | tf_op jit(solution)/shard_map/ppermute | solution.py:581
  237.8 5.8 %collective-permute-start.11 = (bf16[3,32,128]{2,1,0:T(8,128)(2,1)}, bf16[3,32,128]{2,1,0:T(8,128)(2,1)S(1)}, u32[]{:S(2)}, u32[]{:S(2)}) collective-permute-start(bf16[3,32,128]{2,1,0:T(8,128)(2,1)} %get-tuple-element.59), channel_id=1, source_target_pairs={{0,24},{8,16},{16,8},{24,0},{1,25},{9,17},{17,9},{25,1},{2,26},{10... | collective-permute-start | bytes 73736 | tf_op jit(solution)/shard_map/ppermute | solution.py:581
  239.4 5.7 %collective-permute-start.10 = (bf16[3,32,128]{2,1,0:T(8,128)(2,1)S(1)}, bf16[3,32,128]{2,1,0:T(8,128)(2,1)S(1)}, u32[]{:S(2)}, u32[]{:S(2)}) collective-permute-start(bf16[3,32,128]{2,1,0:T(8,128)(2,1)S(1)} %copy-done.7), channel_id=1, source_target_pairs={{0,24},{8,16},{16,8},{24,0},{1,25},{9,17},{17,9},{25,1},{2,26},{10... | collective-permute-start | bytes 73736 | tf_op jit(solution)/shard_map/ppermute | solution.py:581
  241.5 31.3 %collective-permute-start.4 = (bf16[4,4,24,768]{3,2,1,0:T(8,128)(2,1)}, bf16[4,4,24,768]{3,2,1,0:T(8,128)(2,1)S(1)}, u32[]{:S(2)}, u32[]{:S(2)}) collective-permute-start(bf16[4,4,24,768]{3,2,1,0:T(8,128)(2,1)} %get-tuple-element.50), channel_id=1, source_target_pairs={{0,16},{8,24},{16,0},{24,8},{1,17},{9,25},{17,1},{25,9},{2,18},{10... | collective-permute-start | bytes 1769480 | tf_op jit(solution)/shard_map/ppermute | solution.py:581
  242.8 30.0 %collective-permute-start.5 = (bf16[4,4,24,768]{3,2,1,0:T(8,128)(2,1)}, bf16[4,4,24,768]{3,2,1,0:T(8,128)(2,1)S(1)}, u32[]{:S(2)}, u32[]{:S(2)}) collective-permute-start(bf16[4,4,24,768]{3,2,1,0:T(8,128)(2,1)} %get-tuple-element.51), channel_id=1, source_target_pairs={{0,24},{8,16},{16,8},{24,0},{1,25},{9,17},{17,9},{25,1},{2,26},{10... | collective-permute-start | bytes 1769480 | tf_op jit(solution)/shard_map/ppermute | solution.py:581
  243.7 31.1 %collective-permute-start = (bf16[4,4,24,768]{3,2,1,0:T(8,128)(2,1)}, bf16[4,4,24,768]{3,2,1,0:T(8,128)(2,1)S(1)}, u32[]{:S(2)}, u32[]{:S(2)}) collective-permute-start(bf16[4,4,24,768]{3,2,1,0:T(8,128)(2,1)} %get-tuple-element.45), channel_id=1, source_target_pairs={{0,8},{8,0},{16,24},{24,16},{1,9},{9,1},{17,25},{25,17},{2,10},{10... | collective-permute-start | bytes 1769480 | tf_op jit(solution)/shard_map/ppermute | solution.py:581
  245.1 48.5 %collective-permute-start.1 = (bf16[4,4,24,768]{3,2,1,0:T(8,128)(2,1)}, bf16[4,4,24,768]{3,2,1,0:T(8,128)(2,1)S(1)}, u32[]{:S(2)}, u32[]{:S(2)}) collective-permute-start(bf16[4,4,24,768]{3,2,1,0:T(8,128)(2,1)} %get-tuple-element.46), channel_id=1, source_target_pairs={{0,16},{8,24},{16,0},{24,8},{1,17},{9,25},{17,1},{25,9},{2,18},{10... | collective-permute-start | bytes 1769480 | tf_op jit(solution)/shard_map/ppermute | solution.py:581
  246.3 47.3 %collective-permute-start.2 = (bf16[4,4,24,768]{3,2,1,0:T(8,128)(2,1)}, bf16[4,4,24,768]{3,2,1,0:T(8,128)(2,1)}, u32[]{:S(2)}, u32[]{:S(2)}) collective-permute-start(bf16[4,4,24,768]{3,2,1,0:T(8,128)(2,1)} %get-tuple-element.47), channel_id=1, source_target_pairs={{0,24},{8,16},{16,8},{24,0},{1,25},{9,17},{17,9},{25,1},{2,26},{10... | collective-permute-start | bytes 1769480 | tf_op jit(solution)/shard_map/ppermute | solution.py:581
  250.0 43.6 %copy-start.1 = (bf16[4,4,24,768]{3,2,1,0:T(8,128)(2,1)S(1)}, bf16[4,4,24,768]{3,2,1,0:T(8,128)(2,1)}, u32[]{:S(2)}) copy-start(bf16[4,4,24,768]{3,2,1,0:T(8,128)(2,1)} %get-tuple-element.44.refs_0_) | copy-start | bytes 1769476

commit v2 on v1

--- a/solution.py
+++ b/solution.py
@@ -27,7 +27,9 @@
     return (product - turns * period) * (2.0 * math.pi / period)
 
 
-def forward_kernel(bands, waves, x_ref, o_ref, table, coarse, fine):
+def forward_kernel(bands, waves, me_ref, x_ref, *refs):
+    outs = refs[:bands]
+    table, coarse, fine = refs[bands:]
     tracers, band, longitudes = x_ref.shape[1:]
     columns = table.shape[1]
     local = 2 * waves
@@ -37,7 +39,7 @@
     def _():
         def waves_of(rows):
             q = lax.broadcasted_iota(jnp.int32, (rows, columns), 1)
-            p = q // local
+            p = (q // local) ^ me_ref[0]
             part = (q % local) // waves
             wave = bands * (q % waves) + p
             return wave.astype(f32), part
@@ -67,34 +69,42 @@
     y = jnp.dot(x, table[...], preferred_element_type=f32) * (1.0 / longitudes)
     y = y.astype(bf16).reshape(tracers, band, columns)
     for t in range(tracers):
-        for p in range(bands):
-            o_ref[p, :, t * local : (t + 1) * local] = y[t, :, p * local : (p + 1) * local]
-
-
-def forward_transform(x, bands, waves):
+        for k in range(bands):
+            outs[k][:, t * local : (t + 1) * local] = y[t, :, k * local : (k + 1) * local]
+
+
+def forward_transform(me, x, bands, waves):
     group, tracers, band, longitudes = x.shape
     local = 2 * waves
     step = 32 if longitudes % 32 == 0 else 8
     return pl.pallas_call(
         functools.partial(forward_kernel, bands, waves),
-        grid=(group,),
-        in_specs=[pl.BlockSpec((1, tracers, band, longitudes), lambda g: (g, 0, 0, 0))],
-        out_specs=pl.BlockSpec((bands, band, tracers * local), lambda g: (0, 0, g)),
-        out_shape=jax.ShapeDtypeStruct((bands, band, group * tracers * local), bf16),
-        scratch_shapes=[
-            pltpu.VMEM((longitudes, bands * local), bf16),
-            pltpu.VMEM((2, longitudes // step, bands * local), f32),
-            pltpu.VMEM((2, step, bands * local), f32),
-        ],
+        grid_spec=pltpu.PrefetchScalarGridSpec(
+            num_scalar_prefetch=1,
+            grid=(group,),
+            in_specs=[pl.BlockSpec((1, tracers, band, longitudes), lambda g, me: (g, 0, 0, 0))],
+            out_specs=[pl.BlockSpec((band, tracers * local), lambda g, me: (0, g))] * bands,
+            scratch_shapes=[
+                pltpu.VMEM((longitudes, bands * local), bf16),
+                pltpu.VMEM((2, longitudes // step, bands * local), f32),
+                pltpu.VMEM((2, step, bands * local), f32),
+            ],
+        ),
+        out_shape=[jax.ShapeDtypeStruct((band, group * tracers * local), bf16)] * bands,
         compiler_params=pltpu.CompilerParams(vmem_limit_bytes=60 * 2**20),
         name="forward_dft",
-    )(x)
-
-
-def meridional_kernel(waves, a_ref, ahead_ref, back_ref, gain_ref, o_ref):
+    )(me, x)
+
+
+def meridional_kernel(waves, bands, *refs):
+    pieces = refs[:bands]
+    ahead_ref, back_ref, gain_ref, o_ref, arrived = refs[bands:]
     local = 2 * waves
-    tracers = a_ref.shape[1] // local
-    spectrum = jnp.dot(ahead_ref[...], a_ref[...], preferred_element_type=f32)
+    band, columns = pieces[0].shape
+    tracers = columns // local
+    for k in range(bands):
+        arrived[k * band : (k + 1) * band, :] = pieces[k][...]
+    spectrum = jnp.dot(ahead_ref[...], arrived[...], preferred_element_type=f32)
     gain = jnp.concatenate([gain_ref[...]] * tracers, axis=1)
     damped = (spectrum * gain).astype(bf16)
     back = jnp.dot(back_ref[...], damped, preferred_element_type=f32).astype(bf16)
@@ -106,16 +116,18 @@
 
 
 def meridional_transform(arrived, ahead, back, gain, waves, tracers, owners):
-    latitudes, columns = arrived.shape
+    band, columns = arrived[0].shape
+    bands = len(arrived)
+    latitudes = bands * band
     local = 2 * waves
     group = columns // (tracers * local)
     own = latitudes // owners
     whole = lambda g: (0, 0)
     return pl.pallas_call(
-        functools.partial(meridional_kernel, waves),
+        functools.partial(meridional_kernel, waves, bands),
         grid=(group,),
-        in_specs=[
-            pl.BlockSpec((latitudes, tracers * local), lambda g: (0, g)),
+        in_specs=[pl.BlockSpec((band, tracers * local), lambda g: (0, g))] * bands
+        + [
             pl.BlockSpec(ahead.shape, whole),
             pl.BlockSpec(back.shape, whole),
             pl.BlockSpec(gain.shape, whole),
@@ -123,8 +135,14 @@
         out_specs=pl.BlockSpec((owners, 1, tracers * own, local), lambda g: (0, g, 0, 0)),
         out_shape=jax.ShapeDtypeStruct((owners, group, tracers * own, local), bf16),
         compiler_params=pltpu.CompilerParams(vmem_limit_bytes=60 * 2**20),
+        scratch_shapes=[pltpu.VMEM((latitudes, tracers * local), bf16)],
+        cost_estimate=pl.CostEstimate(
+            flops=4 * latitudes * NW * columns,
+            bytes_accessed=4 * latitudes * columns,
+            transcendentals=0,
+        ),
         name="meridional",
-    )(arrived, ahead, back, gain)
+    )(*arrived, ahead, back, gain)
 
 
 def meridional_tables(latitudes, own, bands, groups):
@@ -137,7 +155,10 @@
         angle = theta * order
         return jnp.where(even, jnp.cos(angle), jnp.sin(angle)).astype(bf16)
 
-    theta = (jnp.arange(latitudes, dtype=f32) + 0.5) * (math.pi / latitudes)
+    band = own * groups
+    lat = jnp.arange(latitudes, dtype=jnp.int32)
+    lat = ((lat // band) ^ device) * band + lat % band
+    theta = (lat.astype(f32) + 0.5) * (math.pi / latitudes)
     ahead = values(theta[None, :], order[:, None])
     rows = own // PLAT
     index = (
@@ -513,8 +534,12 @@
     cols = longitudes // PLON
     mem = lax.axis_index("mem")
 
-    fourier = forward_transform(initial_concentrations, bands, waves)
-    arrived = lax.all_to_all(fourier, "grid", split_axis=0, concat_axis=0, tiled=True)
+    place_on_grid = lax.axis_index("grid").astype(jnp.int32).reshape(1)
+    fourier = forward_transform(place_on_grid, initial_concentrations, bands, waves)
+    arrived = []
+    for k, piece in enumerate(fourier):
+        pairs = [(i, i ^ k) for i in range(bands)]
+        arrived.append(piece if k == 0 else lax.ppermute(piece, "grid", pairs))
 
     factors = lax.all_to_all(
         kinetic_scaling_factors.reshape(group, reactions, groups, patch_rows, cols).transpose(
@@ -550,7 +575,7 @@
     variance = own_patches(error_variance)
 
     last = meridional_transform(
-        arrived.reshape(latitudes, group * tracers * 2 * waves),
+        arrived,
         ahead,
         back,
         gain,

time: 298 us -> 291 us (0.977)
  waiting for transfers between devices: 129 us -> 100 us
  starting transfers between devices: 27.1 us -> 48.9 us
    all_to_all x1 -> x0, waiting for transfers between devices: 56.2 us -> none  [on_device(): lax.all_to_all(fourier, 'grid', split_axis=0, concat_axis=0, tiled=True)]
    ppermute x0 -> x7, waiting for transfers between devices: none -> 27 us  [on_device(): arrived.append(piece if k == 0 else lax.ppermute(piece, 'grid', pairs))]
    all_to_all x1, starting transfers between devices: 4.2 us -> 22.5 us  [on_device(): lax.all_to_all(last, ('mem', 'grid'), split_axis=0, concat_axis=0, tiled=...]
    ppermute x0 -> x7, starting transfers between devices: none -> 9.93 us  [on_device(): arrived.append(piece if k == 0 else lax.ppermute(piece, 'grid', pairs))]
    all_to_all x1 -> x0, starting transfers between devices: 6.49 us -> none  [on_device(): lax.all_to_all(fourier, 'grid', split_axis=0, concat_axis=0, tiled=True)]
  transfers between devices with their start and end apart: 15 -> 21, of which waited for: 5 -> 8; matrix products, arithmetic and copies ran while one was open for 21% -> 22% of each run, Pallas kernels for 6% -> 6%
where the time goes in v2:
time: 291 us; the launch traced here: 290 us
  waiting for transfers between devices  100 us (34%)
  Pallas kernels  71.2 us (24%)
  starting transfers between devices  48.9 us (17%)
  other arithmetic  47.8 us (16%)
  local copies, waits for them, and re-layouts  20.7 us (7%)
    ppermute x12, waiting for transfers between devices, on_device(): lax.ppermute(result, 'mem', pairs)  44.7 us
    pallas_call x2, Pallas kernels, chemistry(): pl.pallas_call(chemistry_kernel, grid=(cols,), in_specs=[pl.BlockSpec(z.s...  30.6 us
    all_to_all x1, waiting for transfers between devices, on_device(): lax.all_to_all(last, ('mem', 'grid'), split_axis=0, concat_axis=0, tiled=...  28.4 us
    ppermute x7, waiting for transfers between devices, on_device(): arrived.append(piece if k == 0 else lax.ppermute(piece, 'grid', pairs))  27 us
    convert_element_type x1, other arithmetic, inverse_table(): return (weight * jnp.cos(angle)).astype(bf16)  26.7 us
    all_to_all x1, starting transfers between devices, on_device(): lax.all_to_all(last, ('mem', 'grid'), split_axis=0, concat_axis=0, tiled=...  22.5 us
    pallas_call x2, Pallas kernels, analyse(): pl.pallas_call(functools.partial(analysis_kernel, groups), grid_spec=pltp...  17.3 us
    convert_element_type x2, other arithmetic, values(): return jnp.where(even, jnp.cos(angle), jnp.sin(angle)).astype(bf16)  13.9 us
  transfers between devices with their start and end apart: 21, of which 8 were waited for; matrix products, arithmetic and copies ran while one was open for 22% of the time, Pallas kernels for 6%

profile of v2, /device:TPU:0, one launch (start us, length us, event | category | flops | bytes accessed | tf_op | source)
XLA Modules:
  0.0 289.9 jit_solution(2156725190841179061)
XLA Ops:
  0.6 11.1 %forward_dft.1 = (bf16[96,2048]{1,0:T(8,128)(2,1)}, bf16[96,2048]{1,0:T(8,128)(2,1)}, bf16[96,2048]{1,0:T(8,128)(2,1)}, bf16[96,2048]{1,0:T(8,128)(2,1)}, bf16[9...) custom-call(s32[1]{0:T(128)} %bitcast.1.me_ref, ...), custom_call_target="tpu_custom_call" | custom-call | tf_op jit(solution)/shard_map/forward_dft/pallas_call | solution.py:80
  12.2 2.6 collective-permute-start.1
  14.9 2.8 collective-permute-start.3
  18.9 3.7 %all-to-all-start.1 = ((bf16[4,2,1152]{2,1,0:T(2,128)(2,1)}), bf16[4,2,1152]{2,1,0:T(2,128)(2,1)S(1)}, u32[]{:S(2)}, u32[]{:S(2)}) async-start(bf16[4,2,1152]{2,1,0:T(2,128)(2,1)} %reshape.224), calls=%async_computation.1 | async-start | bytes 36864 | tf_op jit(solution)/shard_map/all_to_all | solution.py:544
  22.9 6.9 %fusion.12.refs_9_ = bf16[768,512]{1,0:T(8,128)(2,1)} fusion(f32[512]{0:T(512)S(1)} %select_convert_fusion, f32[768]{0:T(1024)S(1)} %reshape.221, pred[]{:T(512)S(6)} %eq.68), kind=kLoop, calls=%fused_computation.19 | loop fusion | flops 1179648 | bytes 791553 | tf_op jit(solution)/shard_map/convert_element_type | solution.py:156
  29.8 3.6 %collective-permute-start.5 = (bf16[96,2048]{1,0:T(8,128)(2,1)}, bf16[96,2048]{1,0:T(8,128)(2,1)S(1)}, u32[]{:S(2)}, u32[]{:S(2)}) collective-permute-start(bf16[96,2048]{1,0:T(8,128)(2,1)} %get-tuple-element.45), channel_id=1, source_target_pairs={{0,6},{1,7},{2,4},{3,5},{4,2},{5,3},{6,0},{7,1},{8,14},{9,15},{10,... | collective-permute-start | bytes 1179656 | tf_op jit(solution)/shard_map/ppermute | solution.py:542
  33.4 8.0 %collective-permute-done.1.refs_2_ = bf16[96,2048]{1,0:T(8,128)(2,1)S(1)} collective-permute-done((bf16[96,2048]{1,0:T(8,128)(2,1)}, bf16[96,2048]{1,0:T(8,128)(2,1)S(1)}, u32[]{:S(2)}, u32[]{:S(2)}) %collective-permute-start.1) | collective-permute-done | bytes 393248 | tf_op jit(solution)/shard_map/ppermute | solution.py:542
  42.7 6.9 %fusion.10.refs_8_ = bf16[512,768]{1,0:T(8,128)(2,1)} fusion(f32[512]{0:T(512)S(1)} %select_convert_fusion, f32[768]{0:T(1024)S(1)} %fusion.42, pred[]{:T(512)S(6)} %eq.68), kind=kLoop, calls=%fused_computation.17 | loop fusion | flops 1179648 | bytes 791553 | tf_op jit(solution)/shard_map/convert_element_type | solution.py:156
  50.0 11.3 %collective-permute-done.5.refs_6_ = bf16[96,2048]{1,0:T(8,128)(2,1)S(1)} collective-permute-done((bf16[96,2048]{1,0:T(8,128)(2,1)}, bf16[96,2048]{1,0:T(8,128)(2,1)S(1)}, u32[]{:S(2)}, u32[]{:S(2)}) %collective-permute-start.5) | collective-permute-done | bytes 393248 | tf_op jit(solution)/shard_map/ppermute | solution.py:542
  61.3 7.3 %collective-permute-done.6.refs_7_ = bf16[96,2048]{1,0:T(8,128)(2,1)S(1)} collective-permute-done((bf16[96,2048]{1,0:T(8,128)(2,1)}, bf16[96,2048]{1,0:T(8,128)(2,1)S(1)}, u32[]{:S(2)}, u32[]{:S(2)}) %collective-permute-start.6) | collective-permute-done | bytes 393248 | tf_op jit(solution)/shard_map/ppermute | solution.py:542
  69.4 7.5 %meridional.1 = bf16[32,4,96,128]{3,2,1,0:T(8,128)(2,1)} custom-call(bf16[96,2048]{1,0:T(8,128)(2,1)} %get-tuple-element.39.refs_0_, bf16[96,2048]{1,0:T(8,128)(2,1)} %copy-done.6, bf16[96,2048]{1,0:T(8,128)(2,1)} %copy-done.7, bf16[96,2048]{1,0:T(8,128)(2,1)} %copy-done.8, bf16[96,2048]{1,0:T(8,128)(2,1)} %copy-done.9, bf16[96,2048]{1,0:T(8,128)(2,1)} %copy-done.10, ...), custom_call_target="tpu_custom_call" | custom-call | flops 3221225472 | bytes 6291456 | tf_op jit(solution)/shard_map/meridional/pallas_call | solution.py:126
  76.9 22.5 %all-to-all-start = ((bf16[32,4,96,128]{3,2,1,0:T(8,128)(2,1)}), bf16[32,4,96,128]{3,2,1,0:T(8,128)(2,1)S(1)}, u32[]{:S(2)}, u32[]{:S(2)}) async-start(bf16[32,4,96,128]{3,2,1,0:T(8,128)(2,1)} %meridional.1), calls=%async_computation | async-start | bytes 6291456 | tf_op jit(solution)/shard_map/all_to_all | solution.py:586
  99.4 2.6 dynamic-slice_convert_fusion
  102.0 4.0 %reshape.222 = f32[12,8,3,1536]{3,2,1,0:T(4,128)} reshape(f32[12,24,1536]{2,1,0:T(8,128)} %dynamic-slice_convert_fusion) | data formatting | bytes 3538944 | tf_op jit(solution)/shard_map/transpose | solution.py:560
  106.0 3.4 %copy.43 = f32[12,8,3,1536]{3,1,2,0:T(8,128)} copy(f32[12,8,3,1536]{3,2,1,0:T(4,128)} %reshape.222) | data formatting | bytes 3538944 | tf_op jit(solution)/shard_map/transpose | solution.py:560
  112.1 26.7 %fusion.5.table_ref = bf16[1024,1536]{1,0:T(8,128)(2,1)} fusion(s32[1024]{0:T(1024)S(1)} %get-tuple-element.87, s32[1024]{0:T(1024)S(1)} %get-tuple-element.86, f32[1024]{0:T(1024)S(1)} %compare_select_fusion), kind=kLoop, calls=%fused_computation.6 | loop fusion | flops 18874368 | bytes 3158016 | tf_op jit(solution)/shard_map/convert_element_type | solution.py:197
  140.0 2.5 copy.29
  143.4 28.4 %all-to-all-done = bf16[32,4,96,128]{3,2,1,0:T(8,128)(2,1)S(1)} async-done(((bf16[32,4,96,128]{3,2,1,0:T(8,128)(2,1)}), bf16[32,4,96,128]{3,2,1,0:T(8,128)(2,1)S(1)}, u32[]{:S(2)}, u32[]{:S(2)}) %all-to-all-start) | async-done | bytes 3145760 | tf_op jit(solution)/shard_map/all_to_all | solution.py:586
  171.8 4.3 %broadcast_in_dim.50.factor_ref = f32[6,16,12,8,128]{4,3,2,1,0:T(8,128)} broadcast(f32[6,16,12,8]{3,2,1,0:T(8,128)} %copy.29), dimensions={0,1,2,3} | broadcast | bytes 4755456 | tf_op jit(solution)/shard_map/broadcast_in_dim | solution.py:562
  176.1 15.3 %chemistry.2 = (bf16[4,3,128,768]{3,2,1,0:T(8,128)(2,1)}, f32[3,16,8,128]{3,2,1,0:T(8,128)}) custom-call(bf16[4,8,384,128]{3,2,1,0:T(8,128)(2,1)} %bitcast.77, bf16[1024,1536]{1,0:T(8,128)(2,1)} %fusion.5.table_ref, f32[12,3,8,1536]{3,2,1,0:T(8,128)} %bitcast.79, f32[6,16,12,8,128]{4,3,2,1,0:T(8,128)} %broadcast_in_dim.50.factor_ref, ...), custom_call_target="tpu_custom_call" | custom-call | flops 2415919104 | bytes 25165824 | tf_op jit(solution)/shard_map/chemistry/pallas_call | solution.py:281
  191.4 8.5 %analysis.2 = (bf16[4,4,24,768]{3,2,1,0:T(8,128)(2,1)}, bf16[4,4,24,768]{3,2,1,0:T(8,128)(2,1)}, bf16[4,4,24,768]{3,2,1,0:T(8,128)(2,1)}, bf16[4,4,24,768]{3,2,1...) custom-call(s32[1]{0:T(128)} %bitcast.me_ref, ...), custom_call_target="tpu_custom_call" | custom-call | flops 6000000000 | bytes 9437184 | tf_op jit(solution)/shard_map/analysis/pallas_call | solution.py:436
  200.0 15.3 %chemistry.3 = (bf16[4,3,128,768]{3,2,1,0:T(8,128)(2,1)}, f32[3,16,8,128]{3,2,1,0:T(8,128)}) custom-call(bf16[4,8,384,128]{3,2,1,0:T(8,128)(2,1)} %bitcast.78, bf16[1024,1536]{1,0:T(8,128)(2,1)} %fusion.5.table_ref, f32[12,3,8,1536]{3,2,1,0:T(8,128)} %bitcast.80, f32[6,16,12,8,128]{4,3,2,1,0:T(8,128)} %broadcast_in_dim.50.factor_ref, ...), custom_call_target="tpu_custom_call" | custom-call | flops 2415919104 | bytes 25165824 | tf_op jit(solution)/shard_map/chemistry/pallas_call | solution.py:281
  215.3 8.8 %analysis.3 = (bf16[4,4,24,768]{3,2,1,0:T(8,128)(2,1)}, bf16[4,4,24,768]{3,2,1,0:T(8,128)(2,1)}, bf16[4,4,24,768]{3,2,1,0:T(8,128)(2,1)}, bf16[4,4,24,768]{3,2,1...) custom-call(s32[1]{0:T(128)} %bitcast.me_ref, ...), custom_call_target="tpu_custom_call" | custom-call | flops 6000000000 | bytes 9437184 | tf_op jit(solution)/shard_map/analysis/pallas_call | solution.py:436
  224.1 2.1 collective-permute-start.14
  226.3 1.4 collective-permute-start.16
  228.3 3.0 %collective-permute-done.14 = bf16[3,32,128]{2,1,0:T(8,128)(2,1)S(1)} collective-permute-done((bf16[3,32,128]{2,1,0:T(8,128)(2,1)}, bf16[3,32,128]{2,1,0:T(8,128)(2,1)S(1)}, u32[]{:S(2)}, u32[]{:S(2)}) %collective-permute-start.14) | collective-permute-done | bytes 24608 | tf_op jit(solution)/shard_map/ppermute | solution.py:606
  231.3 1.6 collective-permute-start.18
  241.6 1.8 copy.33
  243.4 22.8 %collective-permute-done.11.refs_2_ = bf16[4,4,24,768]{3,2,1,0:T(8,128)(2,1)S(1)} collective-permute-done((bf16[4,4,24,768]{3,2,1,0:T(8,128)(2,1)}, bf16[4,4,24,768]{3,2,1,0:T(8,128)(2,1)S(1)}, u32[]{:S(2)}, u32[]{:S(2)}) %collective-permute-start.11) | collective-permute-done | bytes 589856 | tf_op jit(solution)/shard_map/ppermute | solution.py:606
  266.3 2.0 assemble.2.refs_4_
  268.2 18.8 %collective-permute-done.8.refs_2_ = bf16[4,4,24,768]{3,2,1,0:T(8,128)(2,1)S(1)} collective-permute-done((bf16[4,4,24,768]{3,2,1,0:T(8,128)(2,1)}, bf16[4,4,24,768]{3,2,1,0:T(8,128)(2,1)S(1)}, u32[]{:S(2)}, u32[]{:S(2)}) %collective-permute-start.8) | collective-permute-done | bytes 589856 | tf_op jit(solution)/shard_map/ppermute | solution.py:606
  287.1 2.7 assemble.3
  (88 shorter events, 18.6 us)
Async XLA Ops:
  0.6 17.0 %copy-start.3 = (bf16[4,12,32,6]{2,0,3,1:T(4,128)(2,1)S(1)}, bf16[4,12,32,6]{2,0,3,1:T(4,128)(2,1)}, u32[]{:S(2)}) copy-start(bf16[4,12,32,6]{2,0,3,1:T(4,128)(2,1)} %param.8) | copy-start | bytes 55300
  11.7 18.1 %collective-permute-start = (bf16[96,2048]{1,0:T(8,128)(2,1)}, bf16[96,2048]{1,0:T(8,128)(2,1)S(1)}, u32[]{:S(2)}, u32[]{:S(2)}) collective-permute-start(bf16[96,2048]{1,0:T(8,128)(2,1)} %get-tuple-element.40), channel_id=1, source_target_pairs={{0,1},{1,0},{2,3},{3,2},{4,5},{5,4},{6,7},{7,6},{8,9},{9,8},{10,11... | collective-permute-start | bytes 1179656 | tf_op jit(solution)/shard_map/ppermute | solution.py:542
  12.2 29.2 %collective-permute-start.1 = (bf16[96,2048]{1,0:T(8,128)(2,1)}, bf16[96,2048]{1,0:T(8,128)(2,1)S(1)}, u32[]{:S(2)}, u32[]{:S(2)}) collective-permute-start(bf16[96,2048]{1,0:T(8,128)(2,1)} %get-tuple-element.41), channel_id=1, source_target_pairs={{0,2},{1,3},{2,0},{3,1},{4,6},{5,7},{6,4},{7,5},{8,10},{9,11},{10,... | collective-permute-start | bytes 1179656 | tf_op jit(solution)/shard_map/ppermute | solution.py:542
  14.9 34.8 %collective-permute-start.2 = (bf16[96,2048]{1,0:T(8,128)(2,1)}, bf16[96,2048]{1,0:T(8,128)(2,1)S(1)}, u32[]{:S(2)}, u32[]{:S(2)}) collective-permute-start(bf16[96,2048]{1,0:T(8,128)(2,1)} %get-tuple-element.42), channel_id=1, source_target_pairs={{0,3},{1,2},{2,1},{3,0},{4,7},{5,6},{6,5},{7,4},{8,11},{9,10},{10,... | collective-permute-start | bytes 1179656 | tf_op jit(solution)/shard_map/ppermute | solution.py:542
  14.9 34.7 %collective-permute-start.3 = (bf16[96,2048]{1,0:T(8,128)(2,1)}, bf16[96,2048]{1,0:T(8,128)(2,1)S(1)}, u32[]{:S(2)}, u32[]{:S(2)}) collective-permute-start(bf16[96,2048]{1,0:T(8,128)(2,1)} %get-tuple-element.43), channel_id=1, source_target_pairs={{0,4},{1,5},{2,6},{3,7},{4,0},{5,1},{6,2},{7,3},{8,12},{9,13},{10,... | collective-permute-start | bytes 1179656 | tf_op jit(solution)/shard_map/ppermute | solution.py:542
  17.7 32.4 %collective-permute-start.4 = (bf16[96,2048]{1,0:T(8,128)(2,1)}, bf16[96,2048]{1,0:T(8,128)(2,1)S(1)}, u32[]{:S(2)}, u32[]{:S(2)}) collective-permute-start(bf16[96,2048]{1,0:T(8,128)(2,1)} %get-tuple-element.44), channel_id=1, source_target_pairs={{0,5},{1,4},{2,7},{3,6},{4,1},{5,0},{6,3},{7,2},{8,13},{9,12},{10,... | collective-permute-start | bytes 1179656 | tf_op jit(solution)/shard_map/ppermute | solution.py:542
  18.9 58.0 %all-to-all-start.1 = ((bf16[4,2,1152]{2,1,0:T(2,128)(2,1)}), bf16[4,2,1152]{2,1,0:T(2,128)(2,1)S(1)}, u32[]{:S(2)}, u32[]{:S(2)}) async-start(bf16[4,2,1152]{2,1,0:T(2,128)(2,1)} %reshape.224), calls=%async_computation.1 | async-start | bytes 36864 | tf_op jit(solution)/shard_map/all_to_all | solution.py:544
  29.8 38.8 %copy-start.6 = (bf16[96,2048]{1,0:T(8,128)(2,1)}, bf16[96,2048]{1,0:T(8,128)(2,1)S(1)}, u32[]{:S(2)}) copy-start(bf16[96,2048]{1,0:T(8,128)(2,1)S(1)} %collective-permute-done.refs_1_) | copy-start | bytes 1179652
  29.8 31.5 %collective-permute-start.5 = (bf16[96,2048]{1,0:T(8,128)(2,1)}, bf16[96,2048]{1,0:T(8,128)(2,1)S(1)}, u32[]{:S(2)}, u32[]{:S(2)}) collective-permute-start(bf16[96,2048]{1,0:T(8,128)(2,1)} %get-tuple-element.45), channel_id=1, source_target_pairs={{0,6},{1,7},{2,4},{3,5},{4,2},{5,3},{6,0},{7,1},{8,14},{9,15},{10,... | collective-permute-start | bytes 1179656 | tf_op jit(solution)/shard_map/ppermute | solution.py:542
  41.4 27.3 %copy-start.7 = (bf16[96,2048]{1,0:T(8,128)(2,1)}, bf16[96,2048]{1,0:T(8,128)(2,1)S(1)}, u32[]{:S(2)}) copy-start(bf16[96,2048]{1,0:T(8,128)(2,1)S(1)} %collective-permute-done.1.refs_2_) | copy-start | bytes 1179652
  41.4 27.3 %collective-permute-start.6 = (bf16[96,2048]{1,0:T(8,128)(2,1)}, bf16[96,2048]{1,0:T(8,128)(2,1)S(1)}, u32[]{:S(2)}, u32[]{:S(2)}) collective-permute-start(bf16[96,2048]{1,0:T(8,128)(2,1)} %get-tuple-element.46), channel_id=1, source_target_pairs={{0,7},{1,6},{2,5},{3,4},{4,3},{5,2},{6,1},{7,0},{8,15},{9,14},{10,... | collective-permute-start | bytes 1179656 | tf_op jit(solution)/shard_map/ppermute | solution.py:542
  49.6 19.1 %copy-start.8 = (bf16[96,2048]{1,0:T(8,128)(2,1)}, bf16[96,2048]{1,0:T(8,128)(2,1)S(1)}, u32[]{:S(2)}) copy-start(bf16[96,2048]{1,0:T(8,128)(2,1)S(1)} %collective-permute-done.2.refs_3_) | copy-start | bytes 1179652
  49.6 19.1 %copy-start.9 = (bf16[96,2048]{1,0:T(8,128)(2,1)}, bf16[96,2048]{1,0:T(8,128)(2,1)S(1)}, u32[]{:S(2)}) copy-start(bf16[96,2048]{1,0:T(8,128)(2,1)S(1)} %collective-permute-done.3.refs_4_) | copy-start | bytes 1179652
  50.0 18.7 %copy-start.10 = (bf16[96,2048]{1,0:T(8,128)(2,1)}, bf16[96,2048]{1,0:T(8,128)(2,1)S(1)}, u32[]{:S(2)}) copy-start(bf16[96,2048]{1,0:T(8,128)(2,1)S(1)} %collective-permute-done.4.refs_5_) | copy-start | bytes 1179652
  76.9 94.8 %all-to-all-start = ((bf16[32,4,96,128]{3,2,1,0:T(8,128)(2,1)}), bf16[32,4,96,128]{3,2,1,0:T(8,128)(2,1)S(1)}, u32[]{:S(2)}, u32[]{:S(2)}) async-start(bf16[32,4,96,128]{3,2,1,0:T(8,128)(2,1)} %meridional.1), calls=%async_computation | async-start | bytes 6291456 | tf_op jit(solution)/shard_map/all_to_all | solution.py:586
  215.3 24.4 %collective-permute-start.10 = (bf16[4,4,24,768]{3,2,1,0:T(8,128)(2,1)}, bf16[4,4,24,768]{3,2,1,0:T(8,128)(2,1)S(1)}, u32[]{:S(2)}, u32[]{:S(2)}) collective-permute-start(bf16[4,4,24,768]{3,2,1,0:T(8,128)(2,1)} %get-tuple-element.65), channel_id=1, source_target_pairs={{0,8},{8,0},{16,24},{24,16},{1,9},{9,1},{17,25},{25,17},{2,10},{10... | collective-permute-start | bytes 1769480 | tf_op jit(solution)/shard_map/ppermute | solution.py:606
  215.3 12.4 %copy-start.14 = (bf16[3,32,128]{2,1,0:T(8,128)(2,1)S(1)}, bf16[3,32,128]{2,1,0:T(8,128)(2,1)}, u32[]{:S(2)}) copy-start(bf16[3,32,128]{2,1,0:T(8,128)(2,1)} %get-tuple-element.72) | copy-start | bytes 73732
  215.3 17.5 %copy-start.13 = (bf16[3,32,128]{2,1,0:T(8,128)(2,1)S(1)}, bf16[3,32,128]{2,1,0:T(8,128)(2,1)}, u32[]{:S(2)}) copy-start(bf16[3,32,128]{2,1,0:T(8,128)(2,1)} %get-tuple-element.74) | copy-start | bytes 73732
  215.3 18.9 %copy-start.5 = (bf16[3,32,128]{2,1,0:T(8,128)(2,1)S(1)}, bf16[3,32,128]{2,1,0:T(8,128)(2,1)}, u32[]{:S(2)}) copy-start(bf16[3,32,128]{2,1,0:T(8,128)(2,1)} %get-tuple-element.68) | copy-start | bytes 73732
  215.3 50.9 %copy-start = (bf16[4,4,24,768]{3,2,1,0:T(8,128)(2,1)S(1)}, bf16[4,4,24,768]{3,2,1,0:T(8,128)(2,1)}, u32[]{:S(2)}) copy-start(bf16[4,4,24,768]{3,2,1,0:T(8,128)(2,1)} %get-tuple-element.64.refs_0_) | copy-start | bytes 1769476
  224.1 7.2 %collective-permute-start.14 = (bf16[3,32,128]{2,1,0:T(8,128)(2,1)}, bf16[3,32,128]{2,1,0:T(8,128)(2,1)S(1)}, u32[]{:S(2)}, u32[]{:S(2)}) collective-permute-start(bf16[3,32,128]{2,1,0:T(8,128)(2,1)} %get-tuple-element.71), channel_id=1, source_target_pairs={{0,8},{8,0},{16,24},{24,16},{1,9},{9,1},{17,25},{25,17},{2,10},{10... | collective-permute-start | bytes 73736 | tf_op jit(solution)/shard_map/ppermute | solution.py:606
  226.2 6.7 %collective-permute-start.13 = (bf16[3,32,128]{2,1,0:T(8,128)(2,1)S(1)}, bf16[3,32,128]{2,1,0:T(8,128)(2,1)S(1)}, u32[]{:S(2)}, u32[]{:S(2)}) collective-permute-start(bf16[3,32,128]{2,1,0:T(8,128)(2,1)S(1)} %copy-done.15), channel_id=1, source_target_pairs={{0,8},{8,0},{16,24},{24,16},{1,9},{9,1},{17,25},{25,17},{2,10},{10... | collective-permute-start | bytes 73736 | tf_op jit(solution)/shard_map/ppermute | solution.py:606
  226.3 8.7 %collective-permute-start.16 = (bf16[3,32,128]{2,1,0:T(8,128)(2,1)}, bf16[3,32,128]{2,1,0:T(8,128)(2,1)S(1)}, u32[]{:S(2)}, u32[]{:S(2)}) collective-permute-start(bf16[3,32,128]{2,1,0:T(8,128)(2,1)} %get-tuple-element.73), channel_id=1, source_target_pairs={{0,16},{8,24},{16,0},{24,8},{1,17},{9,25},{17,1},{25,9},{2,18},{10... | collective-permute-start | bytes 73736 | tf_op jit(solution)/shard_map/ppermute | solution.py:606
  227.7 8.5 %collective-permute-start.15 = (bf16[3,32,128]{2,1,0:T(8,128)(2,1)S(1)}, bf16[3,32,128]{2,1,0:T(8,128)(2,1)S(1)}, u32[]{:S(2)}, u32[]{:S(2)}) collective-permute-start(bf16[3,32,128]{2,1,0:T(8,128)(2,1)S(1)} %copy-done.14), channel_id=1, source_target_pairs={{0,16},{8,24},{16,0},{24,8},{1,17},{9,25},{17,1},{25,9},{2,18},{10... | collective-permute-start | bytes 73736 | tf_op jit(solution)/shard_map/ppermute | solution.py:606
  231.3 5.8 %collective-permute-start.18 = (bf16[3,32,128]{2,1,0:T(8,128)(2,1)}, bf16[3,32,128]{2,1,0:T(8,128)(2,1)S(1)}, u32[]{:S(2)}, u32[]{:S(2)}) collective-permute-start(bf16[3,32,128]{2,1,0:T(8,128)(2,1)} %get-tuple-element.75), channel_id=1, source_target_pairs={{0,24},{8,16},{16,8},{24,0},{1,25},{9,17},{17,9},{25,1},{2,26},{10... | collective-permute-start | bytes 73736 | tf_op jit(solution)/shard_map/ppermute | solution.py:606
  232.8 5.7 %collective-permute-start.17 = (bf16[3,32,128]{2,1,0:T(8,128)(2,1)S(1)}, bf16[3,32,128]{2,1,0:T(8,128)(2,1)S(1)}, u32[]{:S(2)}, u32[]{:S(2)}) collective-permute-start(bf16[3,32,128]{2,1,0:T(8,128)(2,1)S(1)} %copy-done.13), channel_id=1, source_target_pairs={{0,24},{8,16},{16,8},{24,0},{1,25},{9,17},{17,9},{25,1},{2,26},{10... | collective-permute-start | bytes 73736 | tf_op jit(solution)/shard_map/ppermute | solution.py:606
  235.0 31.3 %collective-permute-start.11 = (bf16[4,4,24,768]{3,2,1,0:T(8,128)(2,1)}, bf16[4,4,24,768]{3,2,1,0:T(8,128)(2,1)S(1)}, u32[]{:S(2)}, u32[]{:S(2)}) collective-permute-start(bf16[4,4,24,768]{3,2,1,0:T(8,128)(2,1)} %get-tuple-element.66), channel_id=1, source_target_pairs={{0,16},{8,24},{16,0},{24,8},{1,17},{9,25},{17,1},{25,9},{2,18},{10... | collective-permute-start | bytes 1769480 | tf_op jit(solution)/shard_map/ppermute | solution.py:606
  236.2 30.0 %collective-permute-start.12 = (bf16[4,4,24,768]{3,2,1,0:T(8,128)(2,1)}, bf16[4,4,24,768]{3,2,1,0:T(8,128)(2,1)S(1)}, u32[]{:S(2)}, u32[]{:S(2)}) collective-permute-start(bf16[4,4,24,768]{3,2,1,0:T(8,128)(2,1)} %get-tuple-element.67), channel_id=1, source_target_pairs={{0,24},{8,16},{16,8},{24,0},{1,25},{9,17},{17,9},{25,1},{2,26},{10... | collective-permute-start | bytes 1769480 | tf_op jit(solution)/shard_map/ppermute | solution.py:606
  237.1 31.1 %collective-permute-start.7 = (bf16[4,4,24,768]{3,2,1,0:T(8,128)(2,1)}, bf16[4,4,24,768]{3,2,1,0:T(8,128)(2,1)S(1)}, u32[]{:S(2)}, u32[]{:S(2)}) collective-permute-start(bf16[4,4,24,768]{3,2,1,0:T(8,128)(2,1)} %get-tuple-element.61), channel_id=1, source_target_pairs={{0,8},{8,0},{16,24},{24,16},{1,9},{9,1},{17,25},{25,17},{2,10},{10... | collective-permute-start | bytes 1769480 | tf_op jit(solution)/shard_map/ppermute | solution.py:606
  238.5 48.5 %collective-permute-start.8 = (bf16[4,4,24,768]{3,2,1,0:T(8,128)(2,1)}, bf16[4,4,24,768]{3,2,1,0:T(8,128)(2,1)S(1)}, u32[]{:S(2)}, u32[]{:S(2)}) collective-permute-start(bf16[4,4,24,768]{3,2,1,0:T(8,128)(2,1)} %get-tuple-element.62), channel_id=1, source_target_pairs={{0,16},{8,24},{16,0},{24,8},{1,17},{9,25},{17,1},{25,9},{2,18},{10... | collective-permute-start | bytes 1769480 | tf_op jit(solution)/shard_map/ppermute | solution.py:606
  239.7 47.3 %collective-permute-start.9 = (bf16[4,4,24,768]{3,2,1,0:T(8,128)(2,1)}, bf16[4,4,24,768]{3,2,1,0:T(8,128)(2,1)}, u32[]{:S(2)}, u32[]{:S(2)}) collective-permute-start(bf16[4,4,24,768]{3,2,1,0:T(8,128)(2,1)} %get-tuple-element.63), channel_id=1, source_target_pairs={{0,24},{8,16},{16,8},{24,0},{1,25},{9,17},{17,9},{25,1},{2,26},{10... | collective-permute-start | bytes 1769480 | tf_op jit(solution)/shard_map/ppermute | solution.py:606
  243.4 43.6 %copy-start.1 = (bf16[4,4,24,768]{3,2,1,0:T(8,128)(2,1)S(1)}, bf16[4,4,24,768]{3,2,1,0:T(8,128)(2,1)}, u32[]{:S(2)}) copy-start(bf16[4,4,24,768]{3,2,1,0:T(8,128)(2,1)} %get-tuple-element.60.refs_0_) | copy-start | bytes 1769476
  (5 other events, 30.8 us)

commit v3 on v2

--- a/solution.py
+++ b/solution.py
@@ -14,7 +14,8 @@
 SWEEPS = 5
 LANES = 128
 SUBLANES = 8
-CHUNKS = 2
+CHUNKS = 3
+HALVES = 2
 
 
 damping = 2.0
@@ -73,8 +74,8 @@
             outs[k][:, t * local : (t + 1) * local] = y[t, :, k * local : (k + 1) * local]
 
 
-def forward_transform(me, x, bands, waves):
-    group, tracers, band, longitudes = x.shape
+def forward_transform(me, x, bands, waves, first, group):
+    _, tracers, band, longitudes = x.shape
     local = 2 * waves
     step = 32 if longitudes % 32 == 0 else 8
     return pl.pallas_call(
@@ -82,7 +83,9 @@
         grid_spec=pltpu.PrefetchScalarGridSpec(
             num_scalar_prefetch=1,
             grid=(group,),
-            in_specs=[pl.BlockSpec((1, tracers, band, longitudes), lambda g, me: (g, 0, 0, 0))],
+            in_specs=[
+                pl.BlockSpec((1, tracers, band, longitudes), lambda g, me: (g + first, 0, 0, 0))
+            ],
             out_specs=[pl.BlockSpec((band, tracers * local), lambda g, me: (0, g))] * bands,
             scratch_shapes=[
                 pltpu.VMEM((longitudes, bands * local), bf16),
@@ -92,13 +95,19 @@
         ),
         out_shape=[jax.ShapeDtypeStruct((band, group * tracers * local), bf16)] * bands,
         compiler_params=pltpu.CompilerParams(vmem_limit_bytes=60 * 2**20),
+        cost_estimate=pl.CostEstimate(
+            flops=2 * group * tracers * band * longitudes * bands * local,
+            bytes_accessed=4 * group * tracers * band * longitudes,
+            transcendentals=0,
+        ),
         name="forward_dft",
     )(me, x)
 
 
 def meridional_kernel(waves, bands, *refs):
     pieces = refs[:bands]
-    ahead_ref, back_ref, gain_ref, o_ref, arrived = refs[bands:]
+    ahead_ref, back_ref, gain_ref = refs[bands : bands + 3]
+    o_ref, arrived = refs[-2:]
     local = 2 * waves
     band, columns = pieces[0].shape
     tracers = columns // local
@@ -115,26 +124,28 @@
         o_ref[:, 0, t * own : (t + 1) * own, :] = part
 
 
-def meridional_transform(arrived, ahead, back, gain, waves, tracers, owners):
+def meridional_transform(arrived, ahead, back, gain, waves, tracers, owners, before, first, group):
     band, columns = arrived[0].shape
     bands = len(arrived)
     latitudes = bands * band
     local = 2 * waves
-    group = columns // (tracers * local)
     own = latitudes // owners
     whole = lambda g: (0, 0)
+    extra = [] if before is None else [before]
     return pl.pallas_call(
         functools.partial(meridional_kernel, waves, bands),
-        grid=(group,),
+        grid=(columns // (tracers * local),),
         in_specs=[pl.BlockSpec((band, tracers * local), lambda g: (0, g))] * bands
         + [
             pl.BlockSpec(ahead.shape, whole),
             pl.BlockSpec(back.shape, whole),
             pl.BlockSpec(gain.shape, whole),
-        ],
-        out_specs=pl.BlockSpec((owners, 1, tracers * own, local), lambda g: (0, g, 0, 0)),
+        ]
+        + [pl.BlockSpec(memory_space=pl.ANY)] * len(extra),
+        out_specs=pl.BlockSpec((owners, 1, tracers * own, local), lambda g: (0, g + first, 0, 0)),
         out_shape=jax.ShapeDtypeStruct((owners, group, tracers * own, local), bf16),
         compiler_params=pltpu.CompilerParams(vmem_limit_bytes=60 * 2**20),
+        input_output_aliases={} if before is None else {bands + 3: 0},
         scratch_shapes=[pltpu.VMEM((latitudes, tracers * local), bf16)],
         cost_estimate=pl.CostEstimate(
             flops=4 * latitudes * NW * columns,
@@ -142,7 +153,7 @@
             transcendentals=0,
         ),
         name="meridional",
-    )(*arrived, ahead, back, gain)
+    )(*arrived, ahead, back, gain, *extra)
 
 
 def meridional_tables(latitudes, own, bands, groups):
@@ -535,11 +546,23 @@
     mem = lax.axis_index("mem")
 
     place_on_grid = lax.axis_index("grid").astype(jnp.int32).reshape(1)
-    fourier = forward_transform(place_on_grid, initial_concentrations, bands, waves)
+    place_on_grid = lax.axis_index("grid").astype(jnp.int32).reshape(1)
+    halves = HALVES if group % HALVES == 0 else 1
+    part = group // halves
     arrived = []
-    for k, piece in enumerate(fourier):
-        pairs = [(i, i ^ k) for i in range(bands)]
-        arrived.append(piece if k == 0 else lax.ppermute(piece, "grid", pairs))
+    for half in range(halves):
+        fourier = forward_transform(
+            place_on_grid, initial_concentrations, bands, waves, half * part, part
+        )
+        pieces = []
+        for k, piece in enumerate(fourier):
+            pairs = [(i, i ^ k) for i in range(bands)]
+            pieces.append(piece if k == 0 else lax.ppermute(piece, "grid", pairs))
+        arrived.append(pieces)
+        if half < halves - 1:
+            initial_concentrations, arrived[-1][0] = lax.optimization_barrier(
+                (initial_concentrations, arrived[-1][0])
+            )
 
     factors = lax.all_to_all(
         kinetic_scaling_factors.reshape(group, reactions, groups, patch_rows, cols).transpose(
@@ -574,15 +597,20 @@
     observed = own_patches(measured_value)
     variance = own_patches(error_variance)
 
-    last = meridional_transform(
-        arrived,
-        ahead,
-        back,
-        gain,
-        waves,
-        tracers,
-        groups * bands,
-    )
+    last = None
+    for half in range(halves):
+        last = meridional_transform(
+            arrived[half],
+            ahead,
+            back,
+            gain,
+            waves,
+            tracers,
+            groups * bands,
+            last,
+            half * part,
+            group,
+        )
     returned = lax.all_to_all(last, ("mem", "grid"), split_axis=0, concat_axis=0, tiled=True)
     z = returned.reshape(groups, bands, group * tracers * own, 2 * waves)
     me = mem.astype(jnp.int32).reshape(1)

time: 291 us -> 314 us (1.079)
  Pallas kernels: 71.2 us -> 87.4 us
  starting transfers between devices: 48.9 us -> 58.8 us
  waiting for transfers between devices: 100 us -> 94.8 us
    ppermute x7 -> x14, starting transfers between devices: 9.93 us -> 25 us  [on_device(): pieces.append(piece if k == 0 else lax.ppermute(piece, 'grid', pairs))]
    all_to_all x1, starting transfers between devices: 22.5 us -> 11.4 us  [on_device(): lax.all_to_all(last, ('mem', 'grid'), split_axis=0, concat_axis=0, tiled=...]
    ppermute x7 -> x14, waiting for transfers between devices: 27 us -> 18.9 us  [on_device(): pieces.append(piece if k == 0 else lax.ppermute(piece, 'grid', pairs))]
    ppermute x12 -> x18, starting transfers between devices: 12.8 us -> 18.7 us  [on_device(): lax.ppermute(result, 'mem', pairs)]
    pallas_call x1 -> x2, Pallas kernels: 11.1 us -> 15.6 us  [forward_transform(): pl.pallas_call(functools.partial(forward_kernel, bands, waves), grid_spec...]
    pallas_call x2 -> x3, Pallas kernels: 30.6 us -> 35.1 us  [chemistry(): pl.pallas_call(chemistry_kernel, grid=(cols,), in_specs=[pl.BlockSpec(z.s...]
    pallas_call x2 -> x3, Pallas kernels: 17.3 us -> 21 us  [analyse(): pl.pallas_call(functools.partial(analysis_kernel, groups), grid_spec=pltp...]
    ppermute x12 -> x18, waiting for transfers between devices: 44.7 us -> 47.6 us  [on_device(): lax.ppermute(result, 'mem', pairs)]
  transfers between devices with their start and end apart: 21 -> 34, of which waited for: 8 -> 9; matrix products, arithmetic and copies ran while one was open for 22% -> 20% of each run, Pallas kernels for 6% -> 7%
where the time goes in v3:
time: 314 us; the launch traced here: 313 us
  waiting for transfers between devices  94.8 us (30%)
  Pallas kernels  87.4 us (28%)
  starting transfers between devices  58.8 us (19%)
  other arithmetic  47.8 us (15%)
  local copies, waits for them, and re-layouts  22.6 us (7%)
    ppermute x18, waiting for transfers between devices, on_device(): lax.ppermute(result, 'mem', pairs)  47.6 us
    pallas_call x3, Pallas kernels, chemistry(): pl.pallas_call(chemistry_kernel, grid=(cols,), in_specs=[pl.BlockSpec(z.s...  35.1 us
    all_to_all x1, waiting for transfers between devices, on_device(): lax.all_to_all(last, ('mem', 'grid'), split_axis=0, concat_axis=0, tiled=...  28.3 us
    convert_element_type x1, other arithmetic, inverse_table(): return (weight * jnp.cos(angle)).astype(bf16)  26.7 us
    ppermute x14, starting transfers between devices, on_device(): pieces.append(piece if k == 0 else lax.ppermute(piece, 'grid', pairs))  25 us
    pallas_call x3, Pallas kernels, analyse(): pl.pallas_call(functools.partial(analysis_kernel, groups), grid_spec=pltp...  21 us
    ppermute x14, waiting for transfers between devices, on_device(): pieces.append(piece if k == 0 else lax.ppermute(piece, 'grid', pairs))  18.9 us
    ppermute x18, starting transfers between devices, on_device(): lax.ppermute(result, 'mem', pairs)  18.7 us
  transfers between devices with their start and end apart: 34, of which 9 were waited for; matrix products, arithmetic and copies ran while one was open for 20% of the time, Pallas kernels for 7%

profile of v3, /device:TPU:0, one launch (start us, length us, event | category | flops | bytes accessed | tf_op | source)
XLA Modules:
  0.0 312.9 jit_solution(13704322005330910025)
XLA Ops:
  0.6 7.8 %forward_dft.2 = (bf16[96,1024]{1,0:T(8,128)(2,1)}, bf16[96,1024]{1,0:T(8,128)(2,1)}, bf16[96,1024]{1,0:T(8,128)(2,1)}, bf16[96,1024]{1,0:T(8,128)(2,1)}, bf16[9...) custom-call(s32[1]{0:T(128)} %bitcast.1.me_ref, ...), custom_call_target="tpu_custom_call" | custom-call | flops 2415919104 | bytes 4718592 | tf_op jit(solution)/shard_map/forward_dft/pallas_call | solution.py:81
  8.4 4.1 %collective-permute-start.10 = (bf16[96,1024]{1,0:T(8,128)(2,1)}, bf16[96,1024]{1,0:T(8,128)(2,1)S(1)}, u32[]{:S(2)}, u32[]{:S(2)}) collective-permute-start(bf16[96,1024]{1,0:T(8,128)(2,1)} %get-tuple-element.82), channel_id=1, source_target_pairs={{0,4},{1,5},{2,6},{3,7},{4,0},{5,1},{6,2},{7,3},{8,12},{9,13},{10,... | collective-permute-start | bytes 589832 | tf_op jit(solution)/shard_map/ppermute | solution.py:560
  12.5 3.1 collective-permute-start.12
  17.7 3.7 %all-to-all-start.1 = ((bf16[4,2,1152]{2,1,0:T(2,128)(2,1)}), bf16[4,2,1152]{2,1,0:T(2,128)(2,1)S(1)}, u32[]{:S(2)}, u32[]{:S(2)}) async-start(bf16[4,2,1152]{2,1,0:T(2,128)(2,1)} %reshape.228), calls=%async_computation.1 | async-start | bytes 36864 | tf_op jit(solution)/shard_map/all_to_all | solution.py:567
  21.7 6.9 %fusion.12.refs_9_ = bf16[768,512]{1,0:T(8,128)(2,1)} fusion(f32[512]{0:T(512)S(1)} %select_convert_fusion, f32[768]{0:T(1024)S(1)} %reshape.225, pred[]{:T(512)S(6)} %eq.72), kind=kLoop, calls=%fused_computation.19 | loop fusion | flops 1179648 | bytes 791553 | tf_op jit(solution)/shard_map/convert_element_type | solution.py:167
  28.6 7.8 %forward_dft.3 = (bf16[96,1024]{1,0:T(8,128)(2,1)}, bf16[96,1024]{1,0:T(8,128)(2,1)}, bf16[96,1024]{1,0:T(8,128)(2,1)}, bf16[96,1024]{1,0:T(8,128)(2,1)}, bf16[9...) custom-call(s32[1]{0:T(128)} %bitcast.1.me_ref, ...), custom_call_target="tpu_custom_call" | custom-call | flops 2415919104 | bytes 4718592 | tf_op jit(solution)/shard_map/forward_dft/pallas_call | solution.py:81
  39.7 8.2 %collective-permute-start.1 = (bf16[96,1024]{1,0:T(8,128)(2,1)}, bf16[96,1024]{1,0:T(8,128)(2,1)S(1)}, u32[]{:S(2)}, u32[]{:S(2)}) collective-permute-start(bf16[96,1024]{1,0:T(8,128)(2,1)} %get-tuple-element.72), channel_id=1, source_target_pairs={{0,2},{1,3},{2,0},{3,1},{4,6},{5,7},{6,4},{7,5},{8,10},{9,11},{10,... | collective-permute-start | bytes 589832 | tf_op jit(solution)/shard_map/ppermute | solution.py:560
  47.9 6.9 %fusion.10.refs_8_ = bf16[512,768]{1,0:T(8,128)(2,1)} fusion(f32[512]{0:T(512)S(1)} %select_convert_fusion, f32[768]{0:T(1024)S(1)} %fusion.42, pred[]{:T(512)S(6)} %eq.72), kind=kLoop, calls=%fused_computation.17 | loop fusion | flops 1179648 | bytes 791553 | tf_op jit(solution)/shard_map/convert_element_type | solution.py:167
  54.9 3.2 %collective-permute-start.3 = (bf16[96,1024]{1,0:T(8,128)(2,1)}, bf16[96,1024]{1,0:T(8,128)(2,1)S(1)}, u32[]{:S(2)}, u32[]{:S(2)}) collective-permute-start(bf16[96,1024]{1,0:T(8,128)(2,1)} %get-tuple-element.74), channel_id=1, source_target_pairs={{0,4},{1,5},{2,6},{3,7},{4,0},{5,1},{6,2},{7,3},{8,12},{9,13},{10,... | collective-permute-start | bytes 589832 | tf_op jit(solution)/shard_map/ppermute | solution.py:560
  62.6 5.0 %meridional.2.refs_11_ = bf16[32,4,96,128]{3,2,1,0:T(8,128)(2,1)} custom-call(bf16[96,1024]{1,0:T(8,128)(2,1)} %get-tuple-element.78.refs_0_, bf16[96,1024]{1,0:T(8,128)(2,1)} %copy-done.10, bf16[96,1024]{1,0:T(8,128)(2,1)} %copy-done.11, bf16[96,1024]{1,0:T(8,128)(2,1)} %copy-done.12, bf16[96,1024]{1,0:T(8,128)(2,1)} %copy-done.6, ...), custom_call_target="tpu_custom_call" | custom-call | flops 1610612736 | bytes 3145728 | tf_op jit(solution)/shard_map/meridional/pallas_call | solution.py:135
  67.6 13.3 %collective-permute-done.3.refs_4_ = bf16[96,1024]{1,0:T(8,128)(2,1)S(1)} collective-permute-done((bf16[96,1024]{1,0:T(8,128)(2,1)}, bf16[96,1024]{1,0:T(8,128)(2,1)S(1)}, u32[]{:S(2)}, u32[]{:S(2)}) %collective-permute-start.3) | collective-permute-done | bytes 196640 | tf_op jit(solution)/shard_map/ppermute | solution.py:560
  80.9 4.2 %collective-permute-done.4.refs_5_ = bf16[96,1024]{1,0:T(8,128)(2,1)S(1)} collective-permute-done((bf16[96,1024]{1,0:T(8,128)(2,1)}, bf16[96,1024]{1,0:T(8,128)(2,1)S(1)}, u32[]{:S(2)}, u32[]{:S(2)}) %collective-permute-start.4) | collective-permute-done | bytes 196640 | tf_op jit(solution)/shard_map/ppermute | solution.py:560
  85.9 4.9 %meridional.3 = bf16[32,4,96,128]{3,2,1,0:T(8,128)(2,1)} custom-call(bf16[96,1024]{1,0:T(8,128)(2,1)} %get-tuple-element.70.refs_0_, bf16[96,1024]{1,0:T(8,128)(2,1)} %copy-done.13, bf16[96,1024]{1,0:T(8,128)(2,1)} %copy-done.14, bf16[96,1024]{1,0:T(8,128)(2,1)} %copy-done.15, bf16[96,1024]{1,0:T(8,128)(2,1)} %copy-done.16, ...), custom_call_target="tpu_custom_call", output_to_operand_aliasing={{}: (11, {})} | custom-call | flops 1610612736 | bytes 3145728 | tf_op jit(solution)/shard_map/meridional/pallas_call | solution.py:135
  90.8 11.4 %all-to-all-start = ((bf16[32,4,96,128]{3,2,1,0:T(8,128)(2,1)}), bf16[32,4,96,128]{3,2,1,0:T(8,128)(2,1)S(1)}, u32[]{:S(2)}, u32[]{:S(2)}) async-start(bf16[32,4,96,128]{3,2,1,0:T(8,128)(2,1)} %meridional.3), calls=%async_computation | async-start | bytes 6291456 | tf_op jit(solution)/shard_map/all_to_all | solution.py:614
  102.2 2.6 dynamic-slice_convert_fusion
  104.8 4.0 %reshape.226 = f32[12,8,3,1536]{3,2,1,0:T(4,128)} reshape(f32[12,24,1536]{2,1,0:T(8,128)} %dynamic-slice_convert_fusion) | data formatting | bytes 3538944 | tf_op jit(solution)/shard_map/transpose | solution.py:583
  108.8 3.5 %copy.45 = f32[12,8,3,1536]{3,1,2,0:T(8,128)} copy(f32[12,8,3,1536]{3,2,1,0:T(4,128)} %reshape.226) | data formatting | bytes 3538944 | tf_op jit(solution)/shard_map/transpose | solution.py:583
  115.0 26.7 %fusion.5.table_ref = bf16[1024,1536]{1,0:T(8,128)(2,1)} fusion(s32[1024]{0:T(1024)S(1)} %get-tuple-element.145, s32[1024]{0:T(1024)S(1)} %get-tuple-element.144, f32[1024]{0:T(1024)S(1)} %compare_select_fusion), kind=kLoop, calls=%fused_computation.6 | loop fusion | flops 18874368 | bytes 3158016 | tf_op jit(solution)/shard_map/convert_element_type | solution.py:208
  142.9 2.6 copy.31
  146.3 28.3 %all-to-all-done = bf16[32,4,96,128]{3,2,1,0:T(8,128)(2,1)S(1)} async-done(((bf16[32,4,96,128]{3,2,1,0:T(8,128)(2,1)}), bf16[32,4,96,128]{3,2,1,0:T(8,128)(2,1)S(1)}, u32[]{:S(2)}, u32[]{:S(2)}) %all-to-all-start) | async-done | bytes 3145760 | tf_op jit(solution)/shard_map/all_to_all | solution.py:614
  174.5 4.3 %broadcast_in_dim.50.factor_ref = f32[6,16,12,8,128]{4,3,2,1,0:T(8,128)} broadcast(f32[6,16,12,8]{3,2,1,0:T(8,128)} %copy.31), dimensions={0,1,2,3} | broadcast | bytes 4755456 | tf_op jit(solution)/shard_map/broadcast_in_dim | solution.py:585
  178.9 11.7 %chemistry.3 = (bf16[4,3,128,512]{3,2,1,0:T(8,128)(2,1)}, f32[2,16,8,128]{3,2,1,0:T(8,128)}) custom-call(bf16[4,8,384,128]{3,2,1,0:T(8,128)(2,1)} %bitcast.78, bf16[1024,1536]{1,0:T(8,128)(2,1)} %fusion.5.table_ref, f32[12,3,8,1536]{3,2,1,0:T(8,128)} %bitcast.81, f32[6,16,12,8,128]{4,3,2,1,0:T(8,128)} %broadcast_in_dim.50.factor_ref, ...), custom_call_target="tpu_custom_call" | custom-call | flops 1610612736 | bytes 25165824 | tf_op jit(solution)/shard_map/chemistry/pallas_call | solution.py:292
  190.6 6.9 %analysis.3 = (bf16[4,4,24,512]{3,2,1,0:T(8,128)(2,1)}, bf16[4,4,24,512]{3,2,1,0:T(8,128)(2,1)}, bf16[4,4,24,512]{3,2,1,0:T(8,128)(2,1)}, bf16[4,4,24,512]{3,2,1...) custom-call(s32[1]{0:T(128)} %bitcast.me_ref, ...), custom_call_target="tpu_custom_call" | custom-call | flops 6000000000 | bytes 6291456 | tf_op jit(solution)/shard_map/analysis/pallas_call | solution.py:447
  197.5 11.7 %chemistry.4 = (bf16[4,3,128,512]{3,2,1,0:T(8,128)(2,1)}, f32[2,16,8,128]{3,2,1,0:T(8,128)}) custom-call(bf16[4,8,384,128]{3,2,1,0:T(8,128)(2,1)} %bitcast.79, bf16[1024,1536]{1,0:T(8,128)(2,1)} %fusion.5.table_ref, f32[12,3,8,1536]{3,2,1,0:T(8,128)} %bitcast.82, f32[6,16,12,8,128]{4,3,2,1,0:T(8,128)} %broadcast_in_dim.50.factor_ref, ...), custom_call_target="tpu_custom_call" | custom-call | flops 1610612736 | bytes 25165824 | tf_op jit(solution)/shard_map/chemistry/pallas_call | solution.py:292
  209.2 7.1 %analysis.4 = (bf16[4,4,24,512]{3,2,1,0:T(8,128)(2,1)}, bf16[4,4,24,512]{3,2,1,0:T(8,128)(2,1)}, bf16[4,4,24,512]{3,2,1,0:T(8,128)(2,1)}, bf16[4,4,24,512]{3,2,1...) custom-call(s32[1]{0:T(128)} %bitcast.me_ref, ...), custom_call_target="tpu_custom_call" | custom-call | flops 6000000000 | bytes 6291456 | tf_op jit(solution)/shard_map/analysis/pallas_call | solution.py:447
  216.3 11.7 %chemistry.5 = (bf16[4,3,128,512]{3,2,1,0:T(8,128)(2,1)}, f32[2,16,8,128]{3,2,1,0:T(8,128)}) custom-call(bf16[4,8,384,128]{3,2,1,0:T(8,128)(2,1)} %bitcast.80, bf16[1024,1536]{1,0:T(8,128)(2,1)} %fusion.5.table_ref, f32[12,3,8,1536]{3,2,1,0:T(8,128)} %bitcast.83, f32[6,16,12,8,128]{4,3,2,1,0:T(8,128)} %broadcast_in_dim.50.factor_ref, ...), custom_call_target="tpu_custom_call" | custom-call | flops 1610612736 | bytes 25165824 | tf_op jit(solution)/shard_map/chemistry/pallas_call | solution.py:292
  228.2 7.0 %analysis.5 = (bf16[4,4,24,512]{3,2,1,0:T(8,128)(2,1)}, bf16[4,4,24,512]{3,2,1,0:T(8,128)(2,1)}, bf16[4,4,24,512]{3,2,1,0:T(8,128)(2,1)}, bf16[4,4,24,512]{3,2,1...) custom-call(s32[1]{0:T(128)} %bitcast.me_ref, ...), custom_call_target="tpu_custom_call" | custom-call | flops 6000000000 | bytes 6291456 | tf_op jit(solution)/shard_map/analysis/pallas_call | solution.py:447
  247.1 21.5 %collective-permute-done.31 = bf16[2,32,128]{2,1,0:T(8,128)(2,1)S(1)} collective-permute-done((bf16[2,32,128]{2,1,0:T(8,128)(2,1)}, bf16[2,32,128]{2,1,0:T(8,128)(2,1)S(1)}, u32[]{:S(2)}, u32[]{:S(2)}) %collective-permute-start.31) | collective-permute-done | bytes 16416 | tf_op jit(solution)/shard_map/ppermute | solution.py:634
  269.8 3.5 %collective-permute-done.30 = bf16[2,32,128]{2,1,0:T(8,128)(2,1)S(1)} collective-permute-done((bf16[2,32,128]{2,1,0:T(8,128)(2,1)S(1)}, bf16[2,32,128]{2,1,0:T(8,128)(2,1)S(1)}, u32[]{:S(2)}, u32[]{:S(2)}) %collective-permute-start.30) | collective-permute-done | bytes 16416 | tf_op jit(solution)/shard_map/ppermute | solution.py:634
  274.5 3.7 %collective-permute-done.29 = bf16[2,32,128]{2,1,0:T(8,128)(2,1)S(1)} collective-permute-done((bf16[2,32,128]{2,1,0:T(8,128)(2,1)S(1)}, bf16[2,32,128]{2,1,0:T(8,128)(2,1)S(1)}, u32[]{:S(2)}, u32[]{:S(2)}) %collective-permute-start.29) | collective-permute-done | bytes 16416 | tf_op jit(solution)/shard_map/ppermute | solution.py:634
  290.0 9.1 %collective-permute-done.18.refs_2_ = bf16[4,4,24,512]{3,2,1,0:T(8,128)(2,1)S(1)} collective-permute-done((bf16[4,4,24,512]{3,2,1,0:T(8,128)(2,1)}, bf16[4,4,24,512]{3,2,1,0:T(8,128)(2,1)S(1)}, u32[]{:S(2)}, u32[]{:S(2)}) %collective-permute-start.18) | collective-permute-done | bytes 393248 | tf_op jit(solution)/shard_map/ppermute | solution.py:634
  301.1 9.7 %collective-permute-done.15.refs_2_ = bf16[4,4,24,512]{3,2,1,0:T(8,128)(2,1)S(1)} collective-permute-done((bf16[4,4,24,512]{3,2,1,0:T(8,128)(2,1)}, bf16[4,4,24,512]{3,2,1,0:T(8,128)(2,1)S(1)}, u32[]{:S(2)}, u32[]{:S(2)}) %collective-permute-start.15) | collective-permute-done | bytes 393248 | tf_op jit(solution)/shard_map/ppermute | solution.py:634
  (159 shorter events, 45.6 us)
Async XLA Ops:
  8.4 27.9 %collective-permute-start.10 = (bf16[96,1024]{1,0:T(8,128)(2,1)}, bf16[96,1024]{1,0:T(8,128)(2,1)S(1)}, u32[]{:S(2)}, u32[]{:S(2)}) collective-permute-start(bf16[96,1024]{1,0:T(8,128)(2,1)} %get-tuple-element.82), channel_id=1, source_target_pairs={{0,4},{1,5},{2,6},{3,7},{4,0},{5,1},{6,2},{7,3},{8,12},{9,13},{10,... | collective-permute-start | bytes 589832 | tf_op jit(solution)/shard_map/ppermute | solution.py:560
  12.5 25.3 %collective-permute-start.11 = (bf16[96,1024]{1,0:T(8,128)(2,1)}, bf16[96,1024]{1,0:T(8,128)(2,1)S(1)}, u32[]{:S(2)}, u32[]{:S(2)}) collective-permute-start(bf16[96,1024]{1,0:T(8,128)(2,1)} %get-tuple-element.83), channel_id=1, source_target_pairs={{0,5},{1,4},{2,7},{3,6},{4,1},{5,0},{6,3},{7,2},{8,13},{9,12},{10,... | collective-permute-start | bytes 589832 | tf_op jit(solution)/shard_map/ppermute | solution.py:560
  12.5 26.6 %collective-permute-start.12 = (bf16[96,1024]{1,0:T(8,128)(2,1)}, bf16[96,1024]{1,0:T(8,128)(2,1)S(1)}, u32[]{:S(2)}, u32[]{:S(2)}) collective-permute-start(bf16[96,1024]{1,0:T(8,128)(2,1)} %get-tuple-element.84), channel_id=1, source_target_pairs={{0,6},{1,7},{2,4},{3,5},{4,2},{5,3},{6,0},{7,1},{8,14},{9,15},{10,... | collective-permute-start | bytes 589832 | tf_op jit(solution)/shard_map/ppermute | solution.py:560
  15.6 24.1 %collective-permute-start.13 = (bf16[96,1024]{1,0:T(8,128)(2,1)}, bf16[96,1024]{1,0:T(8,128)(2,1)S(1)}, u32[]{:S(2)}, u32[]{:S(2)}) collective-permute-start(bf16[96,1024]{1,0:T(8,128)(2,1)} %get-tuple-element.85), channel_id=1, source_target_pairs={{0,7},{1,6},{2,5},{3,4},{4,3},{5,2},{6,1},{7,0},{8,15},{9,14},{10,... | collective-permute-start | bytes 589832 | tf_op jit(solution)/shard_map/ppermute | solution.py:560
  16.2 38.7 %collective-permute-start.7 = (bf16[96,1024]{1,0:T(8,128)(2,1)}, bf16[96,1024]{1,0:T(8,128)(2,1)S(1)}, u32[]{:S(2)}, u32[]{:S(2)}) collective-permute-start(bf16[96,1024]{1,0:T(8,128)(2,1)} %get-tuple-element.79), channel_id=1, source_target_pairs={{0,1},{1,0},{2,3},{3,2},{4,5},{5,4},{6,7},{7,6},{8,9},{9,8},{10,11... | collective-permute-start | bytes 589832 | tf_op jit(solution)/shard_map/ppermute | solution.py:560
  17.7 73.1 %all-to-all-start.1 = ((bf16[4,2,1152]{2,1,0:T(2,128)(2,1)}), bf16[4,2,1152]{2,1,0:T(2,128)(2,1)S(1)}, u32[]{:S(2)}, u32[]{:S(2)}) async-start(bf16[4,2,1152]{2,1,0:T(2,128)(2,1)} %reshape.228), calls=%async_computation.1 | async-start | bytes 36864 | tf_op jit(solution)/shard_map/all_to_all | solution.py:567
  36.4 18.4 %collective-permute-start.8 = (bf16[96,1024]{1,0:T(8,128)(2,1)S(1)}, bf16[96,1024]{1,0:T(8,128)(2,1)S(1)}, u32[]{:S(2)}, u32[]{:S(2)}) collective-permute-start(bf16[96,1024]{1,0:T(8,128)(2,1)S(1)} %copy-done.29), channel_id=1, source_target_pairs={{0,2},{1,3},{2,0},{3,1},{4,6},{5,7},{6,4},{7,5},{8,10},{9,11},{10,... | collective-permute-start | bytes 589832 | tf_op jit(solution)/shard_map/ppermute | solution.py:560
  37.8 20.2 %collective-permute-start.9 = (bf16[96,1024]{1,0:T(8,128)(2,1)S(1)}, bf16[96,1024]{1,0:T(8,128)(2,1)S(1)}, u32[]{:S(2)}, u32[]{:S(2)}) collective-permute-start(bf16[96,1024]{1,0:T(8,128)(2,1)S(1)} %copy-done.28), channel_id=1, source_target_pairs={{0,3},{1,2},{2,1},{3,0},{4,7},{5,6},{6,5},{7,4},{8,11},{9,10},{10,... | collective-permute-start | bytes 589832 | tf_op jit(solution)/shard_map/ppermute | solution.py:560
  39.1 19.2 %collective-permute-start = (bf16[96,1024]{1,0:T(8,128)(2,1)}, bf16[96,1024]{1,0:T(8,128)(2,1)S(1)}, u32[]{:S(2)}, u32[]{:S(2)}) collective-permute-start(bf16[96,1024]{1,0:T(8,128)(2,1)} %get-tuple-element.71), channel_id=1, source_target_pairs={{0,1},{1,0},{2,3},{3,2},{4,5},{5,4},{6,7},{7,6},{8,9},{9,8},{10,11... | collective-permute-start | bytes 589832 | tf_op jit(solution)/shard_map/ppermute | solution.py:560
  39.7 20.7 %collective-permute-start.1 = (bf16[96,1024]{1,0:T(8,128)(2,1)}, bf16[96,1024]{1,0:T(8,128)(2,1)S(1)}, u32[]{:S(2)}, u32[]{:S(2)}) collective-permute-start(bf16[96,1024]{1,0:T(8,128)(2,1)} %get-tuple-element.72), channel_id=1, source_target_pairs={{0,2},{1,3},{2,0},{3,1},{4,6},{5,7},{6,4},{7,5},{8,10},{9,11},{10,... | collective-permute-start | bytes 589832 | tf_op jit(solution)/shard_map/ppermute | solution.py:560
  54.8 12.7 %collective-permute-start.2 = (bf16[96,1024]{1,0:T(8,128)(2,1)}, bf16[96,1024]{1,0:T(8,128)(2,1)S(1)}, u32[]{:S(2)}, u32[]{:S(2)}) collective-permute-start(bf16[96,1024]{1,0:T(8,128)(2,1)} %get-tuple-element.73), channel_id=1, source_target_pairs={{0,3},{1,2},{2,1},{3,0},{4,7},{5,6},{6,5},{7,4},{8,11},{9,10},{10,... | collective-permute-start | bytes 589832 | tf_op jit(solution)/shard_map/ppermute | solution.py:560
  54.9 26.0 %collective-permute-start.3 = (bf16[96,1024]{1,0:T(8,128)(2,1)}, bf16[96,1024]{1,0:T(8,128)(2,1)S(1)}, u32[]{:S(2)}, u32[]{:S(2)}) collective-permute-start(bf16[96,1024]{1,0:T(8,128)(2,1)} %get-tuple-element.74), channel_id=1, source_target_pairs={{0,4},{1,5},{2,6},{3,7},{4,0},{5,1},{6,2},{7,3},{8,12},{9,13},{10,... | collective-permute-start | bytes 589832 | tf_op jit(solution)/shard_map/ppermute | solution.py:560
  58.0 27.0 %collective-permute-start.4 = (bf16[96,1024]{1,0:T(8,128)(2,1)}, bf16[96,1024]{1,0:T(8,128)(2,1)S(1)}, u32[]{:S(2)}, u32[]{:S(2)}) collective-permute-start(bf16[96,1024]{1,0:T(8,128)(2,1)} %get-tuple-element.75), channel_id=1, source_target_pairs={{0,5},{1,4},{2,7},{3,6},{4,1},{5,0},{6,3},{7,2},{8,13},{9,12},{10,... | collective-permute-start | bytes 589832 | tf_op jit(solution)/shard_map/ppermute | solution.py:560
  58.4 26.7 %collective-permute-start.5 = (bf16[96,1024]{1,0:T(8,128)(2,1)}, bf16[96,1024]{1,0:T(8,128)(2,1)S(1)}, u32[]{:S(2)}, u32[]{:S(2)}) collective-permute-start(bf16[96,1024]{1,0:T(8,128)(2,1)} %get-tuple-element.76), channel_id=1, source_target_pairs={{0,6},{1,7},{2,4},{3,5},{4,2},{5,3},{6,0},{7,1},{8,14},{9,15},{10,... | collective-permute-start | bytes 589832 | tf_op jit(solution)/shard_map/ppermute | solution.py:560
  60.4 24.7 %collective-permute-start.6 = (bf16[96,1024]{1,0:T(8,128)(2,1)}, bf16[96,1024]{1,0:T(8,128)(2,1)S(1)}, u32[]{:S(2)}, u32[]{:S(2)}) collective-permute-start(bf16[96,1024]{1,0:T(8,128)(2,1)} %get-tuple-element.77), channel_id=1, source_target_pairs={{0,7},{1,6},{2,5},{3,4},{4,3},{5,2},{6,1},{7,0},{8,15},{9,14},{10,... | collective-permute-start | bytes 589832 | tf_op jit(solution)/shard_map/ppermute | solution.py:560
  90.8 83.7 %all-to-all-start = ((bf16[32,4,96,128]{3,2,1,0:T(8,128)(2,1)}), bf16[32,4,96,128]{3,2,1,0:T(8,128)(2,1)S(1)}, u32[]{:S(2)}, u32[]{:S(2)}) async-start(bf16[32,4,96,128]{3,2,1,0:T(8,128)(2,1)} %meridional.3), calls=%async_computation | async-start | bytes 6291456 | tf_op jit(solution)/shard_map/all_to_all | solution.py:614
  235.2 5.6 %collective-permute-start.24 = (bf16[2,32,128]{2,1,0:T(8,128)(2,1)S(1)}, bf16[2,32,128]{2,1,0:T(8,128)(2,1)S(1)}, u32[]{:S(2)}, u32[]{:S(2)}) collective-permute-start(bf16[2,32,128]{2,1,0:T(8,128)(2,1)S(1)} %copy-done.35), channel_id=1, source_target_pairs={{0,8},{8,0},{16,24},{24,16},{1,9},{9,1},{17,25},{25,17},{2,10},{10... | collective-permute-start | bytes 49160 | tf_op jit(solution)/shard_map/ppermute | solution.py:634
  237.3 6.0 %collective-permute-start.28 = (bf16[2,32,128]{2,1,0:T(8,128)(2,1)}, bf16[2,32,128]{2,1,0:T(8,128)(2,1)S(1)}, u32[]{:S(2)}, u32[]{:S(2)}) collective-permute-start(bf16[2,32,128]{2,1,0:T(8,128)(2,1)} %get-tuple-element.130), channel_id=1, source_target_pairs={{0,16},{8,24},{16,0},{24,8},{1,17},{9,25},{17,1},{25,9},{2,18},{10... | collective-permute-start | bytes 49160 | tf_op jit(solution)/shard_map/ppermute | solution.py:634
  238.8 5.5 %collective-permute-start.27 = (bf16[2,32,128]{2,1,0:T(8,128)(2,1)S(1)}, bf16[2,32,128]{2,1,0:T(8,128)(2,1)S(1)}, u32[]{:S(2)}, u32[]{:S(2)}) collective-permute-start(bf16[2,32,128]{2,1,0:T(8,128)(2,1)S(1)} %copy-done.34), channel_id=1, source_target_pairs={{0,16},{8,24},{16,0},{24,8},{1,17},{9,25},{17,1},{25,9},{2,18},{10... | collective-permute-start | bytes 49160 | tf_op jit(solution)/shard_map/ppermute | solution.py:634
  239.4 6.0 %collective-permute-start.26 = (bf16[2,32,128]{2,1,0:T(8,128)(2,1)S(1)}, bf16[2,32,128]{2,1,0:T(8,128)(2,1)S(1)}, u32[]{:S(2)}, u32[]{:S(2)}) collective-permute-start(bf16[2,32,128]{2,1,0:T(8,128)(2,1)S(1)} %copy-done.32), channel_id=1, source_target_pairs={{0,16},{8,24},{16,0},{24,8},{1,17},{9,25},{17,1},{25,9},{2,18},{10... | collective-permute-start | bytes 49160 | tf_op jit(solution)/shard_map/ppermute | solution.py:634
  240.8 37.9 %collective-permute-start.20 = (bf16[4,4,24,512]{3,2,1,0:T(8,128)(2,1)S(1)}, bf16[4,4,24,512]{3,2,1,0:T(8,128)(2,1)S(1)}, u32[]{:S(2)}, u32[]{:S(2)}) collective-permute-start(bf16[4,4,24,512]{3,2,1,0:T(8,128)(2,1)S(1)} %copy-done.27), channel_id=1, source_target_pairs={{0,8},{8,0},{16,24},{24,16},{1,9},{9,1},{17,25},{25,17},{2,10},{10... | collective-permute-start | bytes 1179656 | tf_op jit(solution)/shard_map/ppermute | solution.py:634
  241.9 38.1 %collective-permute-start.21 = (bf16[4,4,24,512]{3,2,1,0:T(8,128)(2,1)S(1)}, bf16[4,4,24,512]{3,2,1,0:T(8,128)(2,1)S(1)}, u32[]{:S(2)}, u32[]{:S(2)}) collective-permute-start(bf16[4,4,24,512]{3,2,1,0:T(8,128)(2,1)S(1)} %copy-done.26), channel_id=1, source_target_pairs={{0,16},{8,24},{16,0},{24,8},{1,17},{9,25},{17,1},{25,9},{2,18},{10... | collective-permute-start | bytes 1179656 | tf_op jit(solution)/shard_map/ppermute | solution.py:634
  243.4 38.4 %collective-permute-start.22 = (bf16[4,4,24,512]{3,2,1,0:T(8,128)(2,1)S(1)}, bf16[4,4,24,512]{3,2,1,0:T(8,128)(2,1)S(1)}, u32[]{:S(2)}, u32[]{:S(2)}) collective-permute-start(bf16[4,4,24,512]{3,2,1,0:T(8,128)(2,1)S(1)} %copy-done.24), channel_id=1, source_target_pairs={{0,24},{8,16},{16,8},{24,0},{1,25},{9,17},{17,9},{25,1},{2,26},{10... | collective-permute-start | bytes 1179656 | tf_op jit(solution)/shard_map/ppermute | solution.py:634
  244.3 38.7 %collective-permute-start.17 = (bf16[4,4,24,512]{3,2,1,0:T(8,128)(2,1)S(1)}, bf16[4,4,24,512]{3,2,1,0:T(8,128)(2,1)S(1)}, u32[]{:S(2)}, u32[]{:S(2)}) collective-permute-start(bf16[4,4,24,512]{3,2,1,0:T(8,128)(2,1)S(1)} %copy-done.25), channel_id=1, source_target_pairs={{0,8},{8,0},{16,24},{24,16},{1,9},{9,1},{17,25},{25,17},{2,10},{10... | collective-permute-start | bytes 1179656 | tf_op jit(solution)/shard_map/ppermute | solution.py:634
  245.4 23.3 %collective-permute-start.31 = (bf16[2,32,128]{2,1,0:T(8,128)(2,1)}, bf16[2,32,128]{2,1,0:T(8,128)(2,1)S(1)}, u32[]{:S(2)}, u32[]{:S(2)}) collective-permute-start(bf16[2,32,128]{2,1,0:T(8,128)(2,1)} %get-tuple-element.133), channel_id=1, source_target_pairs={{0,24},{8,16},{16,8},{24,0},{1,25},{9,17},{17,9},{25,1},{2,26},{10... | collective-permute-start | bytes 49160 | tf_op jit(solution)/shard_map/ppermute | solution.py:634
  268.7 4.6 %collective-permute-start.30 = (bf16[2,32,128]{2,1,0:T(8,128)(2,1)S(1)}, bf16[2,32,128]{2,1,0:T(8,128)(2,1)S(1)}, u32[]{:S(2)}, u32[]{:S(2)}) collective-permute-start(bf16[2,32,128]{2,1,0:T(8,128)(2,1)S(1)} %copy-done.31), channel_id=1, source_target_pairs={{0,24},{8,16},{16,8},{24,0},{1,25},{9,17},{17,9},{25,1},{2,26},{10... | collective-permute-start | bytes 49160 | tf_op jit(solution)/shard_map/ppermute | solution.py:634
  273.3 4.9 %collective-permute-start.29 = (bf16[2,32,128]{2,1,0:T(8,128)(2,1)S(1)}, bf16[2,32,128]{2,1,0:T(8,128)(2,1)S(1)}, u32[]{:S(2)}, u32[]{:S(2)}) collective-permute-start(bf16[2,32,128]{2,1,0:T(8,128)(2,1)S(1)} %copy-done.30), channel_id=1, source_target_pairs={{0,24},{8,16},{16,8},{24,0},{1,25},{9,17},{17,9},{25,1},{2,26},{10... | collective-permute-start | bytes 49160 | tf_op jit(solution)/shard_map/ppermute | solution.py:634
  278.2 20.9 %collective-permute-start.18 = (bf16[4,4,24,512]{3,2,1,0:T(8,128)(2,1)}, bf16[4,4,24,512]{3,2,1,0:T(8,128)(2,1)S(1)}, u32[]{:S(2)}, u32[]{:S(2)}) collective-permute-start(bf16[4,4,24,512]{3,2,1,0:T(8,128)(2,1)} %get-tuple-element.116), channel_id=1, source_target_pairs={{0,16},{8,24},{16,0},{24,8},{1,17},{9,25},{17,1},{25,9},{2,18},{10... | collective-permute-start | bytes 1179656 | tf_op jit(solution)/shard_map/ppermute | solution.py:634
  278.7 20.4 %collective-permute-start.19 = (bf16[4,4,24,512]{3,2,1,0:T(8,128)(2,1)}, bf16[4,4,24,512]{3,2,1,0:T(8,128)(2,1)S(1)}, u32[]{:S(2)}, u32[]{:S(2)}) collective-permute-start(bf16[4,4,24,512]{3,2,1,0:T(8,128)(2,1)} %get-tuple-element.117), channel_id=1, source_target_pairs={{0,24},{8,16},{16,8},{24,0},{1,25},{9,17},{17,9},{25,1},{2,26},{10... | collective-permute-start | bytes 1179656 | tf_op jit(solution)/shard_map/ppermute | solution.py:634
  280.0 21.1 %collective-permute-start.14 = (bf16[4,4,24,512]{3,2,1,0:T(8,128)(2,1)}, bf16[4,4,24,512]{3,2,1,0:T(8,128)(2,1)S(1)}, u32[]{:S(2)}, u32[]{:S(2)}) collective-permute-start(bf16[4,4,24,512]{3,2,1,0:T(8,128)(2,1)} %get-tuple-element.111), channel_id=1, source_target_pairs={{0,8},{8,0},{16,24},{24,16},{1,9},{9,1},{17,25},{25,17},{2,10},{10... | collective-permute-start | bytes 1179656 | tf_op jit(solution)/shard_map/ppermute | solution.py:634
  282.5 28.3 %collective-permute-start.15 = (bf16[4,4,24,512]{3,2,1,0:T(8,128)(2,1)}, bf16[4,4,24,512]{3,2,1,0:T(8,128)(2,1)S(1)}, u32[]{:S(2)}, u32[]{:S(2)}) collective-permute-start(bf16[4,4,24,512]{3,2,1,0:T(8,128)(2,1)} %get-tuple-element.112), channel_id=1, source_target_pairs={{0,16},{8,24},{16,0},{24,8},{1,17},{9,25},{17,1},{25,9},{2,18},{10... | collective-permute-start | bytes 1179656 | tf_op jit(solution)/shard_map/ppermute | solution.py:634
  283.0 27.8 %collective-permute-start.16 = (bf16[4,4,24,512]{3,2,1,0:T(8,128)(2,1)}, bf16[4,4,24,512]{3,2,1,0:T(8,128)(2,1)S(1)}, u32[]{:S(2)}, u32[]{:S(2)}) collective-permute-start(bf16[4,4,24,512]{3,2,1,0:T(8,128)(2,1)} %get-tuple-element.113), channel_id=1, source_target_pairs={{0,24},{8,16},{16,8},{24,0},{1,25},{9,17},{17,9},{25,1},{2,26},{10... | collective-permute-start | bytes 1179656 | tf_op jit(solution)/shard_map/ppermute | solution.py:634
  (38 other events, 521.9 us)
